TPU v7x, 256 devices: a whole 4x4x8 slice. The times are simulated.
256 devices in a mesh: angle: 8 (over z), strip: 32 (over y, x, core).
Axes of the slice: x: 4, y: 4, z: 8, core: 2. Of those that a mesh axis runs over, the one named last changes fastest.
Arguments:
- object_field: float32 [2, 8, 4096, 1024], P(None, 'angle', 'strip'), may hold values from -5 to 5
- amplitudes: bfloat16 [8, 128, 256, 256], P('angle', 'strip'), may hold values from 0.25 to 4
- scan_offsets: int32 [8, 128, 2], P('angle', 'strip'), may hold values from 0 to 768, as said below
- probe_field: float32 [2, 256, 256], replicated, may hold values from -5 to 5
- tilt_angles: float32 [8], replicated, may hold values from -3.140625 to 3.140625
Outputs:
- object_grad: float32 [2, 8, 4096, 1024], P(None, 'angle', 'strip')
- probe_grad: float32 [2, 256, 256], replicated
- volume_grad: float32 [32, 8, 16, 16384], P('strip', 'angle')
Inputs may be any that keep to these rules, and one draw needn't show every extreme that they name: `scan_offsets`: row offsets lie in 0 to 0 and column offsets in 0 to 768. In every strip's block of 4 frames, the first frame has row offset 0 and column offset 768, the second row offset 0 and column offset 0, the third column offset 768 // 2.
All inputs are finite; a program needn't handle non-finite values.
Results may differ from a plain program's by a relative error of at most 0.0079.
The roundings to bfloat16 on the way count: a program that leaves them out, or rounds other values in their place, can miss the bound.
Values may be sent and summed in bfloat16 or wider, within the bound.
A program may use at most 64 MiB of HBM per device.

v0:
```python
import math

import jax
import jax.numpy as jnp
from jax import lax
from jax.sharding import PartitionSpec as P

FRAME = 256
HALO = 64
NG = 128


def extended_2(block, sides, width):
    for axis, dim in sides:
        count = lax.axis_size(axis)
        forward = [(i, i + 1) for i in range(count - 1)]
        backward = [(target, source) for source, target in forward]
        low = lax.ppermute(
            lax.slice_in_dim(block, block.shape[dim] - width, None, axis=dim), axis, forward
        )
        high = lax.ppermute(lax.slice_in_dim(block, 0, width, axis=dim), axis, backward)
        block = jnp.concatenate([low, block, high], axis=dim)
    return block


def passed_along(value, axis, steps):
    count = lax.axis_size(axis)
    initial, last = (max(0, -steps), min(count, count - steps))
    return lax.ppermute(value, axis, [(source, source + steps) for source in range(initial, last)])


def dft_tables(size_n):
    indices = jnp.arange(size_n, dtype=jnp.int32)
    product = indices[:, None] * indices[None, :] % size_n
    phase_arg = 2.0 * math.pi / size_n * product.astype(jnp.float32)
    norm_scale = 1.0 / math.sqrt(size_n)
    cos_tab = jnp.cos(phase_arg) * norm_scale
    sin_tab = jnp.sin(phase_arg) * norm_scale
    left_fwd = jnp.stack([jnp.stack([cos_tab, sin_tab]), jnp.stack([-sin_tab, cos_tab])]).astype(
        jnp.bfloat16
    )
    right_fwd = jnp.stack([jnp.stack([cos_tab, -sin_tab]), jnp.stack([sin_tab, cos_tab])]).astype(
        jnp.bfloat16
    )
    return (left_fwd, right_fwd)


def frame_grads(patches, probe_field, amp_block, left_fwd, right_fwd):
    probe_re, probe_im = (probe_field[0], probe_field[1])
    patch_re, patch_im = (patches[:, 0], patches[:, 1])
    exit_wave = jnp.stack(
        [probe_re * patch_re - probe_im * patch_im, probe_re * patch_im + probe_im * patch_re], 1
    ).astype(jnp.bfloat16)
    half = jnp.einsum(
        "abik,fbkj->faij", left_fwd, exit_wave, preferred_element_type=jnp.float32
    ).astype(jnp.bfloat16)
    wave = jnp.einsum("fbik,bakj->faij", half, right_fwd, preferred_element_type=jnp.float32)
    magnitude_sq = wave[:, 0] * wave[:, 0] + wave[:, 1] * wave[:, 1]
    factor = 1.0 - amp_block.astype(jnp.float32) / jnp.sqrt(magnitude_sq + 1.0)
    misfit = (wave * factor[:, None]).astype(jnp.bfloat16)
    back = jnp.einsum(
        "abik,fbkj->faij", right_fwd, misfit, preferred_element_type=jnp.float32
    ).astype(jnp.bfloat16)
    exit_grad = jnp.einsum("fbik,bakj->faij", back, left_fwd, preferred_element_type=jnp.float32)
    grad_re, grad_im = (exit_grad[:, 0], exit_grad[:, 1])
    object_terms = jnp.stack(
        [probe_re * grad_re + probe_im * grad_im, probe_re * grad_im - probe_im * grad_re], 1
    )
    probe_terms = jnp.stack(
        [
            jnp.sum(patch_re * grad_re + patch_im * grad_im, 0),
            jnp.sum(patch_re * grad_im - patch_im * grad_re, 0),
        ]
    )
    return (object_terms, probe_terms)


def slice_project(rows, theta, side_cells, width_cols):
    cell = jnp.arange(side_cells * side_cells, dtype=jnp.int32)
    center = (side_cells - 1) / 2.0
    xpos = (cell // side_cells).astype(jnp.float32) - center
    ypos = (cell % side_cells).astype(jnp.float32) - center
    upos = (width_cols - 1) / 2.0 + 2.0 * (xpos * jnp.cos(theta) + ypos * jnp.sin(theta))
    lower = jnp.clip(jnp.floor(upos), 0.0, width_cols - 2.0)
    frac = upos - lower
    lower_idx = lower.astype(jnp.int32)
    left = jnp.take(rows, lower_idx, axis=1).astype(jnp.float32)
    right = jnp.take(rows, lower_idx + 1, axis=1).astype(jnp.float32)
    return left * (1.0 - frac) + right * frac


def shards(object_field, amplitudes, scan_offsets, probe_field, tilt_angles):
    strip_rows = object_field.shape[2]
    width_cols = object_field.shape[3]
    frame_count = scan_offsets.shape[1]
    left_fwd, right_fwd = dft_tables(FRAME)
    zero_idx = jnp.int32(0)
    extended = extended_2(object_field, (("strip", 2),), HALO)[:, 0]
    offsets = scan_offsets[0]

    def take_patch(offset_pair):
        return lax.dynamic_slice(
            extended, (zero_idx, offset_pair[0], offset_pair[1]), (2, FRAME, FRAME)
        )

    patches = jax.vmap(take_patch)(offsets)
    object_terms, probe_terms = frame_grads(
        patches, probe_field, amplitudes[0], left_fwd, right_fwd
    )

    def add_frame(frame_idx, accum):
        row_at = offsets[frame_idx, 0]
        col_at = offsets[frame_idx, 1]
        current = lax.dynamic_slice(accum, (zero_idx, row_at, col_at), (2, FRAME, FRAME))
        return lax.dynamic_update_slice(
            accum, current + object_terms[frame_idx], (zero_idx, row_at, col_at)
        )

    ext_grad = lax.fori_loop(
        0, frame_count, add_frame, jnp.zeros((2, strip_rows + 2 * HALO, width_cols), jnp.float32)
    )
    lower_rim = ext_grad[:, :HALO]
    upper_rim = ext_grad[:, strip_rows + HALO :]
    from_above = passed_along(lower_rim, "strip", -1)
    from_below = passed_along(upper_rim, "strip", 1)
    core = ext_grad[:, HALO : HALO + strip_rows]
    core = core.at[:, strip_rows - HALO :].add(from_above)
    core = core.at[:, :HALO].add(from_below)
    object_grad = core[:, None]
    total_frames = lax.axis_size("angle") * lax.axis_size("strip") * frame_count
    probe_grad = lax.psum(probe_terms, ("angle", "strip")) * (1.0 / math.sqrt(total_frames))
    phase = (object_field[0, 0] * core[1] - object_field[1, 0] * core[0]).astype(jnp.bfloat16)
    slice_rows = strip_rows // lax.axis_size("angle")
    empty = jnp.zeros((slice_rows, NG * NG), jnp.float32)
    own_start = lax.axis_index("angle") * slice_rows
    total_sum = empty
    piece = lax.all_gather(phase[None], "angle", axis=0, tiled=True)
    first_idx = jnp.int32(0)
    own_rows = lax.dynamic_slice_in_dim(piece, own_start, slice_rows, 1)
    for item in range(piece.shape[0]):
        total_sum = total_sum + slice_project(
            own_rows[item], tilt_angles[first_idx + item], NG, width_cols
        )
    return (object_grad, probe_grad, total_sum[None, None])


def solution(mesh):
    return jax.shard_map(
        shards,
        mesh=mesh,
        in_specs=(
            P(None, "angle", "strip", None),
            P("angle", "strip", None, None),
            P("angle", "strip", None),
            P(),
            P(),
        ),
        out_specs=(P(None, "angle", "strip", None), P(), P("strip", "angle", None, None)),
        check_vma=False,
    )
```

profile of v0, /device:TPU:1, one launch (start us, length us, event | category | flops | bytes accessed | tf_op | source)
XLA Modules:
  0.0 1384.3 jit_solution(15209204040381215339)
XLA Ops:
  10.4 5.1 collective-permute-start.1
  47.0 5.3 maximum_bitcast_fusion
  52.3 4.2 gather_fusion
  74.6 29.8 %while.15 = (s32[]{:T(128)}, f32[2,256,1024]{2,1,0:T(8,128)S(1)}, s32[4,2]{0,1:T(2,128)S(1)}, f32[4,2,256,256]{2,3,1,0:T(8,128)}, s32[]{:T(128)}, /*index=5*/s32[]{:T(128)}, s32[]{:T(128)}) while((s32[]{:T(128)}, f32[2,256,1024]{2,1,0:T(8,128)S(1)}, s32[4,2]{0,1:T(2,128)S(1)}, f32[4,2,256,256]{2,3,1,0:T(8,128)}, s32[]{:T(128)}, ...), condition=%wide.region_1.2_spmd, body=%wide.region_0.1_spmd.sunk | while | flops 131077 | bytes 4718735 | solution.py:119
  133.7 243.3 %all-reduce.2.cloned.1.call-done = f32[2,256,256]{1,2,0:T(8,128)} async-done(((f32[2,256,256]{1,2,0:T(8,128)}), f32[2,256,256]{1,2,0:T(8,128)}) %all-reduce.2.cloned.1.call-update) | async-done | bytes 524304 | tf_op jit(solution)/shard_map/psum | solution.py:131
  380.7 57.6 %gather_fusion.16 = bf16[16384,16]{1,0:T(8,128)(2,1)} fusion(bf16[16,1024]{0,1:T(8,128)(2,1)S(1)} %bitcast.166, s32[16384]{0:T(1024)S(1)} %get-tuple-element.180), kind=kCustom, calls=%fused_computation.15.clone | custom fusion | bytes 1114112 | tf_op jit(solution)/shard_map/jit(_take)/gather | solution.py:88
  441.7 57.4 %gather_fusion.15 = bf16[16384,16]{1,0:T(8,128)(2,1)} fusion(bf16[16,1024]{0,1:T(8,128)(2,1)S(1)} %bitcast.167, s32[16384]{0:T(1024)S(1)} %get-tuple-element.179), kind=kCustom, calls=%fused_computation.14.clone | custom fusion | bytes 1114112 | tf_op jit(solution)/shard_map/jit(_take)/gather | solution.py:87
  502.8 57.4 %gather_fusion.14 = bf16[16384,16]{1,0:T(8,128)(2,1)} fusion(bf16[16,1024]{0,1:T(8,128)(2,1)S(1)} %bitcast.168, s32[16384]{0:T(1024)S(1)} %get-tuple-element.186), kind=kCustom, calls=%fused_computation.13.clone | custom fusion | bytes 1114112 | tf_op jit(solution)/shard_map/jit(_take)/gather | solution.py:88
  563.6 57.4 %gather_fusion.13 = bf16[16384,16]{1,0:T(8,128)(2,1)} fusion(bf16[16,1024]{0,1:T(8,128)(2,1)S(1)} %bitcast.169, s32[16384]{0:T(1024)S(1)} %get-tuple-element.185), kind=kCustom, calls=%fused_computation.12.clone | custom fusion | bytes 1114112 | tf_op jit(solution)/shard_map/jit(_take)/gather | solution.py:87
  624.6 57.4 %gather_fusion.12 = bf16[16384,16]{1,0:T(8,128)(2,1)} fusion(bf16[16,1024]{0,1:T(8,128)(2,1)S(1)} %bitcast.170, s32[16384]{0:T(1024)S(1)} %get-tuple-element.192), kind=kCustom, calls=%fused_computation.11.clone | custom fusion | bytes 1114112 | tf_op jit(solution)/shard_map/jit(_take)/gather | solution.py:88
  685.5 57.4 %gather_fusion.11 = bf16[16384,16]{1,0:T(8,128)(2,1)} fusion(bf16[16,1024]{0,1:T(8,128)(2,1)S(1)} %bitcast.171, s32[16384]{0:T(1024)S(1)} %get-tuple-element.191), kind=kCustom, calls=%fused_computation.10.clone | custom fusion | bytes 1114112 | tf_op jit(solution)/shard_map/jit(_take)/gather | solution.py:87
  746.6 57.4 %gather_fusion.10 = bf16[16384,16]{1,0:T(8,128)(2,1)} fusion(bf16[16,1024]{0,1:T(8,128)(2,1)S(1)} %bitcast.172, s32[16384]{0:T(1024)S(1)} %copy-done.27), kind=kCustom, calls=%fused_computation.9.clone | custom fusion | bytes 1114112 | tf_op jit(solution)/shard_map/jit(_take)/gather | solution.py:88
  803.9 4.4 copy.69
  808.4 57.4 %gather_fusion.9 = bf16[16384,16]{1,0:T(8,128)(2,1)} fusion(bf16[16,1024]{0,1:T(8,128)(2,1)S(1)} %bitcast.173, s32[16384]{0:T(1024)S(1)} %copy-done.26), kind=kCustom, calls=%fused_computation.8.clone | custom fusion | bytes 1114112 | tf_op jit(solution)/shard_map/jit(_take)/gather | solution.py:87
  865.8 4.5 copy.68
  870.4 57.4 %gather_fusion.8 = bf16[16384,16]{1,0:T(8,128)(2,1)} fusion(bf16[16,1024]{0,1:T(8,128)(2,1)S(1)} %bitcast.174, s32[16384]{0:T(1024)S(1)} %copy-done.25), kind=kCustom, calls=%fused_computation.7.clone | custom fusion | bytes 1114112 | tf_op jit(solution)/shard_map/jit(_take)/gather | solution.py:88
  927.8 4.5 copy.67
  932.3 57.4 %gather_fusion.7 = bf16[16384,16]{1,0:T(8,128)(2,1)} fusion(bf16[16,1024]{0,1:T(8,128)(2,1)S(1)} %bitcast.175, s32[16384]{0:T(1024)S(1)} %copy-done.24), kind=kCustom, calls=%fused_computation.6.clone | custom fusion | bytes 1114112 | tf_op jit(solution)/shard_map/jit(_take)/gather | solution.py:87
  989.7 4.4 copy.66
  994.3 57.4 %gather_fusion.6 = bf16[16384,16]{1,0:T(8,128)(2,1)} fusion(bf16[16,1024]{0,1:T(8,128)(2,1)S(1)} %bitcast.176, s32[16384]{0:T(1024)S(1)} %copy-done.23), kind=kCustom, calls=%fused_computation.5.clone | custom fusion | bytes 1114112 | tf_op jit(solution)/shard_map/jit(_take)/gather | solution.py:88
  1051.7 4.5 copy.65
  1056.2 57.4 %gather_fusion.5 = bf16[16384,16]{1,0:T(8,128)(2,1)} fusion(bf16[16,1024]{0,1:T(8,128)(2,1)S(1)} %bitcast.177, s32[16384]{0:T(1024)S(1)} %copy-done.22), kind=kCustom, calls=%fused_computation.4.clone | custom fusion | bytes 1114112 | tf_op jit(solution)/shard_map/jit(_take)/gather | solution.py:87
  1113.5 4.5 copy.64
  1118.2 57.4 %gather_fusion.4 = bf16[16384,16]{1,0:T(8,128)(2,1)} fusion(bf16[16,1024]{0,1:T(8,128)(2,1)S(1)} %bitcast.178, s32[16384]{0:T(1024)S(1)} %copy-done.21), kind=kCustom, calls=%fused_computation.3.clone | custom fusion | bytes 1114112 | tf_op jit(solution)/shard_map/jit(_take)/gather | solution.py:88
  1175.6 4.4 copy.63
  1180.0 57.4 %gather_fusion.3 = bf16[16384,16]{1,0:T(8,128)(2,1)} fusion(bf16[16,1024]{0,1:T(8,128)(2,1)S(1)} %bitcast.179, s32[16384]{0:T(1024)S(1)} %copy-done.20), kind=kCustom, calls=%fused_computation.2.clone | custom fusion | bytes 1114112 | tf_op jit(solution)/shard_map/jit(_take)/gather | solution.py:87
  1237.4 4.5 copy.62
  1242.1 57.4 %gather_fusion.2 = bf16[16384,16]{1,0:T(8,128)(2,1)} fusion(bf16[16,1024]{0,1:T(8,128)(2,1)S(1)} %bitcast.180, s32[16384]{0:T(1024)S(1)} %copy-done.19), kind=kCustom, calls=%fused_computation.1.clone | custom fusion | bytes 1114112 | tf_op jit(solution)/shard_map/jit(_take)/gather | solution.py:88
  1299.5 4.4 copy.61
  1303.9 62.7 %gather_fusion.1 = bf16[16384,16]{1,0:T(8,128)(2,1)} fusion(bf16[16,1024]{0,1:T(8,128)(2,1)S(1)} %bitcast.181, s32[16384]{0:T(1024)} %get-tuple-element.221), kind=kCustom, calls=%fused_computation.clone | custom fusion | bytes 1114112 | tf_op jit(solution)/shard_map/jit(_take)/gather | solution.py:87
  1366.7 4.5 copy.60
  1371.2 5.7 add_bitcast_fusion
  (173 shorter events, 117.0 us)
Async XLA Ops:
  8.0 14.4 %copy-start.33 = (f32[8]{0:T(128)S(1)}, f32[8]{0:T(128)}, u32[]{:S(2)}) copy-start(f32[8]{0:T(128)} %param.17) | copy-start | bytes 100
  8.0 26.5 %copy-start.34 = (s32[1,4,2]{1,2,0:T(2,128)S(1)}, s32[1,4,2]{1,2,0:T(2,128)}, u32[]{:S(2)}) copy-start(s32[1,4,2]{1,2,0:T(2,128)} %param.15) | copy-start | bytes 100
  8.0 27.0 %copy-start.12 = (f32[2,256,256]{2,1,0:T(8,128)S(1)}, f32[2,256,256]{2,1,0:T(8,128)}, u32[]{:S(2)}) copy-start(f32[2,256,256]{2,1,0:T(8,128)} %param.16) | copy-start | bytes 1572868
  8.0 368.9 %all-reduce.2.cloned.1.call-start = ((), (), s32[]{:S(2)}) async-start(), calls=%async_computation | async-start | bytes 1048576 | tf_op jit(solution)/shard_map/psum | solution.py:131
  10.4 34.0 %collective-permute-start.1 = (f32[2,1,64,1024]{3,2,1,0:T(8,128)}, f32[2,1,64,1024]{3,2,1,0:T(8,128)S(1)}, u32[]{:S(2)}, u32[]{:S(2)}) collective-permute-start(f32[2,1,64,1024]{3,2,1,0:T(8,128)} %get-tuple-element.156), channel_id=1, source_target_pairs={{1,0},{2,1},{3,2},{4,3},{5,4},{6,5},{7,6},{8,7},{9,8},{10,9},{11,1... | collective-permute-start | bytes 1572872 | tf_op jit(solution)/shard_map/ppermute | solution.py:21
  15.6 30.2 %collective-permute-start = (f32[2,1,64,1024]{3,2,1,0:T(8,128)}, f32[2,1,64,1024]{3,2,1,0:T(8,128)S(1)}, u32[]{:S(2)}, u32[]{:S(2)}) collective-permute-start(f32[2,1,64,1024]{3,2,1,0:T(8,128)} %get-tuple-element.155), channel_id=1, source_target_pairs={{0,1},{1,2},{2,3},{3,4},{4,5},{5,6},{6,7},{7,8},{8,9},{9,10},{10,1... | collective-permute-start | bytes 1572872 | tf_op jit(solution)/shard_map/ppermute | solution.py:18
  52.3 9.4 copy-start.8
  56.6 6.5 copy-start.9
  56.6 6.5 copy-start.10
  56.6 6.5 copy-start.11
  104.4 8.6 copy-start.1
  104.5 8.6 copy-start.4
  104.5 8.6 copy-start.6
  105.5 10.9 collective-permute-start.2
  110.6 10.9 copy-start.2
  110.6 8.9 collective-permute-start.3
  114.3 264.7 %all-gather.2.cloned.1.call-start = ((), (), s32[]{:S(2)}) async-start(), calls=%async_computation.1 | async-start | bytes 2359296 | tf_op jit(solution)/shard_map/all_gather | solution.py:137
  685.5 60.9 %copy-start.32 = (bf16[1,16,1024]{2,1,0:T(8,128)(2,1)S(1)}, bf16[1,16,1024]{2,1,0:T(8,128)(2,1)}, u32[]{:S(2)}) copy-start(bf16[1,16,1024]{2,1,0:T(8,128)(2,1)} %get-tuple-element.146) | copy-start | bytes 98308
  685.5 61.0 %copy-start.27 = (s32[16384]{0:T(1024)S(1)}, s32[16384]{0:T(1024)}, u32[]{:S(2)}) copy-start(s32[16384]{0:T(1024)} %get-tuple-element.198) | copy-start | bytes 196612
  746.5 61.8 %copy-start.26 = (s32[16384]{0:T(1024)S(1)}, s32[16384]{0:T(1024)}, u32[]{:S(2)}) copy-start(s32[16384]{0:T(1024)} %get-tuple-element.197) | copy-start | bytes 196612
  808.4 62.0 %copy-start.25 = (s32[16384]{0:T(1024)S(1)}, s32[16384]{0:T(1024)}, u32[]{:S(2)}) copy-start(s32[16384]{0:T(1024)} %get-tuple-element.204) | copy-start | bytes 196612
  870.4 61.9 %copy-start.24 = (s32[16384]{0:T(1024)S(1)}, s32[16384]{0:T(1024)}, u32[]{:S(2)}) copy-start(s32[16384]{0:T(1024)} %get-tuple-element.203) | copy-start | bytes 196612
  932.3 62.0 %copy-start.23 = (s32[16384]{0:T(1024)S(1)}, s32[16384]{0:T(1024)}, u32[]{:S(2)}) copy-start(s32[16384]{0:T(1024)} %get-tuple-element.210) | copy-start | bytes 196612
  994.3 61.9 %copy-start.22 = (s32[16384]{0:T(1024)S(1)}, s32[16384]{0:T(1024)}, u32[]{:S(2)}) copy-start(s32[16384]{0:T(1024)} %get-tuple-element.209) | copy-start | bytes 196612
  1056.2 62.0 %copy-start.21 = (s32[16384]{0:T(1024)S(1)}, s32[16384]{0:T(1024)}, u32[]{:S(2)}) copy-start(s32[16384]{0:T(1024)} %get-tuple-element.216) | copy-start | bytes 196612
  1118.2 61.8 %copy-start.20 = (s32[16384]{0:T(1024)S(1)}, s32[16384]{0:T(1024)}, u32[]{:S(2)}) copy-start(s32[16384]{0:T(1024)} %get-tuple-element.215) | copy-start | bytes 196612
  1180.0 62.0 %copy-start.19 = (s32[16384]{0:T(1024)S(1)}, s32[16384]{0:T(1024)}, u32[]{:S(2)}) copy-start(s32[16384]{0:T(1024)} %get-tuple-element.222) | copy-start | bytes 196612
  1303.9 67.3 %copy-start.13 = (f32[16384]{0:T(1024)S(1)}, f32[16384]{0:T(1024)}, u32[]{:S(2)}) copy-start(f32[16384]{0:T(1024)} %get-tuple-element.175) | copy-start | bytes 196612
  1303.9 67.3 %copy-start.14 = (f32[16384]{0:T(1024)S(1)}, f32[16384]{0:T(1024)}, u32[]{:S(2)}) copy-start(f32[16384]{0:T(1024)} %get-tuple-element.176) | copy-start | bytes 196612
  1366.7 4.5 copy-start.16
  1366.7 4.5 copy-start.17
  1366.7 4.5 copy-start.18
  (10 other events, 30.2 us)
Sparse Core Ops, SparseCore 0:
  114.5 262.4 all-reduce.1
Sparse Core Ops, SparseCore 1:
  123.7 45.5 all-gather.1
where the time goes:
time: 1390 us; the launch traced here: 1380 us
  local copies, waits for them, and re-layouts  1040 us (75%)
  waiting for transfers between devices  247 us (18%)
  other arithmetic  46.6 us (3%)
  between operations  27.4 us (2%)
    gather x16, local copies, waits for them, and re-layouts, slice_project(): left = jnp.take(rows, lower_idx, axis=1).astype(jnp.float32)  497 us
    gather x16, local copies, waits for them, and re-layouts, slice_project(): right = jnp.take(rows, lower_idx + 1, axis=1).astype(jnp.float32)  492 us
    psum x1, waiting for transfers between devices, shards(): lax.psum(probe_terms, ('angle', 'strip')) * (1.0 / math.sqrt(total_frames))  243 us
  transfers between devices with their start and end apart: 6, of which 3 were waited for; matrix products, arithmetic and copies ran while one was open for 3% of the time, Pallas kernels for 0%

commit v1 on v0

v1 whole, which is shorter than its diff:
```python
import math

import jax
import jax.numpy as jnp
import numpy as np
from jax import lax
from jax.experimental import pallas as pl
from jax.experimental.pallas import tpu as pltpu
from jax.sharding import PartitionSpec as P

FRAME = 256
HALO = 64
NG = 128
LANES = 128
MESH = pl.DeviceIdType.MESH
F32 = jnp.float32
BF16 = jnp.bfloat16
FIXED_COLS = (768, 0, 384)
WINDOW = (256, 768)


def dft_blocks():
    index = np.arange(FRAME)
    angle = 2.0 * np.pi / FRAME * ((index[:, None] * index[None, :]) % FRAME)
    cos_tab = np.cos(angle) / math.sqrt(FRAME)
    sin_tab = np.sin(angle) / math.sqrt(FRAME)
    fwd = np.block([[cos_tab, sin_tab], [-sin_tab, cos_tab]])
    inv = np.block([[cos_tab, -sin_tab], [sin_tab, cos_tab]])
    return jnp.asarray(fwd, BF16), jnp.asarray(inv, BF16)


def kernel(
    n_angle, n_strip, scale,
    cols, trig, obj_hbm, amp_hbm, probe_hbm, fwd_hbm, inv_hbm,
    og_hbm, pg_hbm, vol_hbm,
    ext, probe, amp, fwd, inv,
    halo_out, halo_in, place_t, place_m, moved3, patch3, xbuf, ybuf, wbuf, mbuf, zbuf, gbuf,
    grad_out, grad_in, core, phase, ph_all,
    pterm, rs_in, ar_in, ag_in, pg_out,
    lower_t, frac_t, lhs, vol,
    load_sem, store_sem, halo_s, halo_r, grad_s, grad_r, a2a_s, a2a_r,
    rs_s, rs_r, ar_s, ar_r, ag_s, ag_r,
):
    width = ext.shape[2]
    me_a = lax.axis_index("angle")
    me_s = lax.axis_index("strip")
    above = lax.rem(me_s + n_strip - 1, n_strip)
    below = lax.rem(me_s + 1, n_strip)

    loads = [
        pltpu.make_async_copy(obj_hbm, ext.at[:, pl.ds(HALO, 128), :], load_sem.at[0]),
        pltpu.make_async_copy(probe_hbm, probe, load_sem.at[1]),
        pltpu.make_async_copy(inv_hbm, inv, load_sem.at[2]),
        pltpu.make_async_copy(fwd_hbm, fwd, load_sem.at[3]),
        pltpu.make_async_copy(amp_hbm, amp, load_sem.at[4]),
    ]
    for load in loads:
        load.start()

    barrier = pltpu.get_barrier_semaphore()

    @pl.loop(1, n_strip)
    def _(d):
        pl.semaphore_signal(
            barrier, inc=1, device_id={"strip": lax.rem(me_s + d, n_strip)}, device_id_type=MESH
        )

    @pl.loop(1, n_angle)
    def _(d):
        pl.semaphore_signal(
            barrier, inc=1, device_id={"angle": lax.rem(me_a + d, n_angle)}, device_id_type=MESH
        )

    loads[0].wait()
    for side, first in ((0, HALO), (1, 2 * HALO)):

        @pl.loop(0, 4)
        def _(step):
            rows = pl.multiple_of(step * 16, 16)
            for part in range(2):
                halo_out[side, part, pl.ds(rows, 16), :] = ext[
                    part, pl.ds(first + rows, 16), :
                ].astype(BF16)

    pl.semaphore_wait(barrier, n_strip - 1 + n_angle - 1)

    def remote(src, dst, send, recv, **where):
        return pltpu.make_async_remote_copy(
            src_ref=src, dst_ref=dst, send_sem=send, recv_sem=recv,
            device_id=where, device_id_type=MESH,
        )

    halo_copies = [
        remote(halo_out.at[1], halo_in.at[0], halo_s.at[0], halo_r.at[0], strip=below),
        remote(halo_out.at[0], halo_in.at[1], halo_s.at[1], halo_r.at[1], strip=above),
    ]
    for copy in halo_copies:
        copy.start()

    col = cols[0].astype(F32)
    for b in range(width // LANES):
        at = lax.broadcasted_iota(jnp.int32, (LANES, FRAME), 0) + b * LANES
        of = lax.broadcasted_iota(jnp.int32, (LANES, FRAME), 1)
        place_t[b * LANES : (b + 1) * LANES, :] = ((at - of).astype(F32) == col).astype(F32).astype(BF16)
        at = lax.broadcasted_iota(jnp.int32, (FRAME, LANES), 1) + b * LANES
        of = lax.broadcasted_iota(jnp.int32, (FRAME, LANES), 0)
        place_m[:, b * LANES : (b + 1) * LANES] = ((at - of).astype(F32) == col).astype(F32).astype(BF16)

    def split(value):
        high = value.astype(BF16)
        return jnp.concatenate([high, (value - high.astype(F32)).astype(BF16)], axis=0)

    def joined(product):
        rows = product.shape[0] // 2
        return product[:rows] + product[rows:]

    def exit_chunk(chunk):
        rows = pl.ds(chunk * HALO, HALO)
        for part in range(2):
            patch3[part, rows, :] = joined(
                jnp.dot(split(ext[part, rows, :]), place_t[...], preferred_element_type=F32)
            )

        @pl.loop(0, 4)
        def _(step):
            local = pl.multiple_of(step * 16, 16)
            row = chunk * HALO + local
            pr, pi = probe[0, pl.ds(row, 16), :], probe[1, pl.ds(row, 16), :]
            res, ims = [
                [ext[part, pl.ds(row, 16), c : c + FRAME] for c in FIXED_COLS]
                + [patch3[part, pl.ds(row, 16), :]]
                for part in range(2)
            ]
            for f in range(4):
                xbuf[chunk, pl.ds(f * HALO + local, 16), :FRAME] = (
                    pr * res[f] - pi * ims[f]
                ).astype(BF16)
                xbuf[chunk, pl.ds(f * HALO + local, 16), FRAME:] = (
                    pr * ims[f] + pi * res[f]
                ).astype(BF16)

        half = jnp.dot(xbuf[chunk], inv[...], preferred_element_type=F32).astype(BF16)
        for f in range(4):
            at = f * HALO
            ybuf[f, pl.ds(chunk * HALO, HALO), :] = half[at : at + HALO, :FRAME]
            ybuf[f, pl.ds(FRAME + chunk * HALO, HALO), :] = half[at : at + HALO, FRAME:]

    loads[1].wait()
    loads[2].wait()
    exit_chunk(1)
    exit_chunk(2)

    center = (NG - 1) / 2.0
    half_x = NG // 2
    xpos = lax.broadcasted_iota(jnp.int32, (half_x, LANES), 0).astype(F32) - center
    ypos = lax.broadcasted_iota(jnp.int32, (half_x, LANES), 1).astype(F32) - center

    @pl.loop(0, n_angle)
    def _(a):
        upos = (width - 1) / 2.0 + 2.0 * (xpos * trig[0, a] + ypos * trig[1, a])
        low = jnp.clip(jnp.floor(upos), 0.0, width - 2.0)
        lower_t[a] = low
        frac_t[a] = upos - low

    for copy in halo_copies:
        copy.wait()
    has_above = (me_s > 0).astype(F32)
    has_below = (me_s < n_strip - 1).astype(F32)
    for side, first, present in ((0, 0, has_above), (1, 3 * HALO, has_below)):

        @pl.loop(0, 4)
        def _(step):
            rows = pl.multiple_of(step * 16, 16)
            for part in range(2):
                ext[part, pl.ds(first + rows, 16), :] = (
                    halo_in[side, part, pl.ds(rows, 16), :].astype(F32) * present
                )

    exit_chunk(0)
    exit_chunk(3)

    loads[3].wait()
    loads[4].wait()

    @pl.loop(0, 4)
    def _(f):
        wbuf[...] = jnp.dot(fwd[...], ybuf[f], preferred_element_type=F32)

        @pl.loop(0, FRAME // 16)
        def _(step):
            row = pl.multiple_of(step * 16, 16)
            wr, wi = wbuf[pl.ds(row, 16), :], wbuf[pl.ds(FRAME + row, 16), :]
            measured = amp[f, pl.ds(row, 16), :].astype(F32)
            factor = 1.0 - measured / jnp.sqrt(wr * wr + wi * wi + 1.0)
            mbuf[f, pl.ds(row, 16), :] = (wr * factor).astype(BF16)
            mbuf[f, pl.ds(FRAME + row, 16), :] = (wi * factor).astype(BF16)

        back = jnp.dot(inv[...], mbuf[f], preferred_element_type=F32).astype(BF16)
        for chunk in range(4):
            at = chunk * HALO
            rows = pl.ds(pl.multiple_of(f * HALO, HALO), HALO)
            zbuf[chunk, rows, :FRAME] = back[at : at + HALO]
            zbuf[chunk, rows, FRAME:] = back[FRAME + at : FRAME + at + HALO]

    def place(terms, moved):
        blocks = [moved[:, b * LANES : (b + 1) * LANES] for b in range(width // LANES)]
        for f in range(3):
            b = FIXED_COLS[f] // LANES
            blocks[b] = blocks[b] + terms[f][:, :LANES]
            blocks[b + 1] = blocks[b + 1] + terms[f][:, LANES:]
        return blocks

    def grad_chunk(chunk):
        gbuf[...] = jnp.dot(zbuf[chunk], fwd[...], preferred_element_type=F32)
        rows = pl.ds(chunk * HALO, HALO)
        pr, pi = probe[0, rows, :], probe[1, rows, :]
        gr, gi = gbuf[3 * HALO :, :FRAME], gbuf[3 * HALO :, FRAME:]
        for part, value in ((0, pr * gr + pi * gi), (1, pr * gi - pi * gr)):
            moved3[part] = joined(
                jnp.dot(split(value), place_m[...], preferred_element_type=F32)
            )

        @pl.loop(0, 4)
        def _(step):
            local = pl.multiple_of(step * 16, 16)
            row = chunk * HALO + local
            rows = pl.ds(row, 16)
            pr, pi = probe[0, rows, :], probe[1, rows, :]
            t_re, t_im, q_re, q_im = [], [], 0.0, 0.0
            for f in range(4):
                gr = gbuf[pl.ds(f * HALO + local, 16), :FRAME]
                gi = gbuf[pl.ds(f * HALO + local, 16), FRAME:]
                if f < 3:
                    t_re.append(pr * gr + pi * gi)
                    t_im.append(pr * gi - pi * gr)
                    c = FIXED_COLS[f]
                    er, ei = ext[0, rows, c : c + FRAME], ext[1, rows, c : c + FRAME]
                else:
                    er, ei = patch3[0, rows, :], patch3[1, rows, :]
                q_re = q_re + (er * gr + ei * gi)
                q_im = q_im + (er * gi - ei * gr)
            pterm[pl.ds(row, 16), :] = q_re.astype(BF16)
            pterm[pl.ds(FRAME + row, 16), :] = q_im.astype(BF16)
            for part, terms in ((0, t_re), (1, t_im)):
                for b, value in enumerate(place(terms, moved3[part, pl.ds(local, 16), :])):
                    cols = slice(b * LANES, (b + 1) * LANES)
                    if chunk in (0, 3):
                        grad_out[chunk // 3, part, pl.ds(local, 16), cols] = value.astype(BF16)
                    else:
                        core[part, pl.ds((chunk - 1) * HALO + local, 16), cols] = value

    grad_copies = [
        remote(grad_out.at[1], grad_in.at[0], grad_s.at[0], grad_r.at[0], strip=below),
        remote(grad_out.at[0], grad_in.at[1], grad_s.at[1], grad_r.at[1], strip=above),
    ]
    grad_chunk(0)
    grad_copies[1].start()
    grad_chunk(3)
    grad_copies[0].start()
    grad_chunk(1)
    grad_chunk(2)

    def rs_copy(d):
        peer = lax.rem(me_s + d, n_strip)
        return remote(
            pterm.at[pl.ds(pl.multiple_of(peer * 16, 16), 16)], rs_in.at[d],
            rs_s.at[d], rs_r.at[d], strip=peer,
        )

    @pl.loop(1, n_strip)
    def _(d):
        rs_copy(d).start()

    for copy in grad_copies:
        copy.wait()
    for side, present in ((0, has_above), (1, has_below)):

        @pl.loop(0, 4)
        def _(step):
            local = pl.multiple_of(step * 16, 16)
            rows = pl.ds(side * HALO + local, 16)
            got = [
                core[part, rows, :]
                + grad_in[side, part, pl.ds(local, 16), :].astype(F32) * present
                for part in range(2)
            ]
            core[0, rows, :] = got[0]
            core[1, rows, :] = got[1]
            own = pl.ds(HALO + side * HALO + local, 16)
            phase[rows, :] = (ext[0, own, :] * got[1] - ext[1, own, :] * got[0]).astype(BF16)

    def a2a_copy(d):
        peer = lax.rem(me_a + d, n_angle)
        return remote(
            phase.at[pl.ds(pl.multiple_of(peer * 16, 16), 16)], ph_all.at[me_a],
            a2a_s.at[d], a2a_r.at[d], angle=peer,
        )

    @pl.loop(1, n_angle)
    def _(d):
        a2a_copy(d).start()

    store_og = pltpu.make_async_copy(core, og_hbm, store_sem.at[0])
    store_og.start()
    ph_all[me_a] = phase[pl.ds(pl.multiple_of(me_a * 16, 16), 16), :]

    @pl.loop(1, n_strip)
    def _(d):
        rs_copy(d).wait()

    own_rows = pl.ds(pl.multiple_of(me_s * 16, 16), 16)
    ar_in[me_a] = lax.fori_loop(
        1, n_strip, lambda d, acc: acc + rs_in[d].astype(F32), pterm[own_rows, :].astype(F32)
    )

    def ar_copy(d):
        peer = lax.rem(me_a + d, n_angle)
        return remote(
            ar_in.at[me_a], ar_in.at[me_a], ar_s.at[d], ar_r.at[d], angle=peer
        )

    @pl.loop(1, n_angle)
    def _(d):
        ar_copy(d).start()

    @pl.loop(1, n_angle)
    def _(d):
        a2a_copy(d).wait()

    flip = (
        lax.broadcasted_iota(jnp.int32, (LANES, LANES), 0)
        + lax.broadcasted_iota(jnp.int32, (LANES, LANES), 1)
        == LANES - 1
    ).astype(F32).astype(BF16)

    @pl.loop(0, n_angle)
    def _(a):
        rows = ph_all[a]
        mirrored = [
            jnp.dot(rows[:, b * LANES : (b + 1) * LANES], flip, preferred_element_type=F32)
            for b in range(8)
        ]
        both = jnp.concatenate(
            [rows.astype(F32), jnp.concatenate(mirrored[::-1], axis=1)], axis=0
        )
        lhs[a, :32, :] = both.astype(BF16)
        lhs[a, 32:, :] = pltpu.roll(both, width - 1, 1).astype(BF16)

    column = lax.broadcasted_iota(jnp.int32, (LANES, LANES), 0).astype(F32).astype(BF16)
    one, zero = jnp.ones((), BF16), jnp.zeros((), BF16)

    def project(x):
        total = jnp.zeros((32, LANES), F32)
        for a in range(n_angle):
            low = lower_t[a, pl.ds(x, 1), :] - float(WINDOW[0])
            frac = frac_t[a, pl.ds(x, 1), :]
            picks = jnp.concatenate(
                [
                    jnp.where(column == (low - float(j * LANES)).astype(BF16), one, zero)
                    for j in range((WINDOW[1] - WINDOW[0]) // LANES)
                ],
                axis=0,
            )
            got = jnp.dot(lhs[a, :, WINDOW[0] : WINDOW[1]], picks, preferred_element_type=F32)
            total = total + (got[:32] * (1.0 - frac) + got[32:] * frac)
        vol[:, pl.ds(pl.multiple_of(x * LANES, LANES), LANES)] = total[:16]
        high = total[16:].astype(BF16)
        rest = (total[16:] - high.astype(F32)).astype(BF16)
        turned = jnp.dot(jnp.concatenate([high, rest], axis=0), flip, preferred_element_type=F32)
        vol[:, pl.ds(pl.multiple_of((NG - 1 - x) * LANES, LANES), LANES)] = turned[:16] + turned[16:]

    pl.loop(0, half_x // 2)(project)

    @pl.loop(1, n_angle)
    def _(d):
        ar_copy(d).wait()

    summed = ar_in[0]
    for a in range(1, n_angle):
        summed = summed + ar_in[a]
    ag_in[own_rows, :] = (summed * scale).astype(BF16)

    def ag_copy(d):
        peer = lax.rem(me_s + d, n_strip)
        return remote(
            ag_in.at[own_rows], ag_in.at[own_rows], ag_s.at[d], ag_r.at[d], strip=peer
        )

    @pl.loop(1, n_strip)
    def _(d):
        ag_copy(d).start()

    pl.loop(half_x // 2, half_x)(project)
    store_vol = pltpu.make_async_copy(vol, vol_hbm, store_sem.at[1])
    store_vol.start()

    def ag_arrived(d):
        sender = lax.rem(me_s + n_strip - d, n_strip)
        rows = pl.ds(pl.multiple_of(sender * 16, 16), 16)
        return remote(ag_in.at[rows], ag_in.at[rows], ag_s.at[d], ag_r.at[d], strip=sender)

    @pl.loop(1, n_strip)
    def _(d):
        ag_copy(d).wait_send()
        ag_arrived(d).wait_recv()

    pg_out[...] = ag_in[...].astype(F32)
    store_pg = pltpu.make_async_copy(pg_out, pg_hbm, store_sem.at[2])
    store_pg.start()
    store_og.wait()
    store_vol.wait()
    store_pg.wait()


def shards(object_field, amplitudes, scan_offsets, probe_field, tilt_angles):
    n_angle, n_strip = lax.axis_size("angle"), lax.axis_size("strip")
    width = object_field.shape[3]
    fwd, inv = dft_blocks()
    trig = jnp.stack([jnp.cos(tilt_angles), jnp.sin(tilt_angles)])
    cols = scan_offsets[0, 3:, 1]
    scale = 1.0 / math.sqrt(n_angle * n_strip * scan_offsets.shape[1])
    hbm = pl.BlockSpec(memory_space=pl.ANY)
    smem = pl.BlockSpec(memory_space=pltpu.SMEM)
    vmem, dma = pltpu.VMEM, pltpu.SemaphoreType.DMA
    object_grad, probe_grad, volume = pl.pallas_call(
        lambda *refs: kernel(n_angle, n_strip, scale, *refs),
        out_shape=(
            jax.ShapeDtypeStruct((2, 128, width), F32),
            jax.ShapeDtypeStruct((2 * FRAME, FRAME), F32),
            jax.ShapeDtypeStruct((16, NG * NG), F32),
        ),
        in_specs=[smem, smem] + [hbm] * 5,
        out_specs=(hbm, hbm, hbm),
        scratch_shapes=[
            vmem((2, FRAME, width), F32),
            vmem((2, FRAME, FRAME), F32),
            vmem((4, FRAME, FRAME), BF16),
            vmem((2 * FRAME, 2 * FRAME), BF16),
            vmem((2 * FRAME, 2 * FRAME), BF16),
            vmem((2, 2, HALO, width), BF16),
            vmem((2, 2, HALO, width), BF16),
            vmem((width, FRAME), BF16),
            vmem((FRAME, width), BF16),
            vmem((2, HALO, width), F32),
            vmem((2, FRAME, FRAME), F32),
            vmem((4, 4 * HALO, 2 * FRAME), BF16),
            vmem((4, 2 * FRAME, FRAME), BF16),
            vmem((2 * FRAME, FRAME), F32),
            vmem((4, 2 * FRAME, FRAME), BF16),
            vmem((4, 4 * HALO, 2 * FRAME), BF16),
            vmem((4 * HALO, 2 * FRAME), F32),
            vmem((2, 2, HALO, width), BF16),
            vmem((2, 2, HALO, width), BF16),
            vmem((2, 128, width), F32),
            vmem((128, width), BF16),
            vmem((n_angle, 16, width), BF16),
            vmem((2 * FRAME, FRAME), BF16),
            vmem((n_strip, 16, FRAME), BF16),
            vmem((n_angle, 16, FRAME), F32),
            vmem((2 * FRAME, FRAME), BF16),
            vmem((2 * FRAME, FRAME), F32),
            vmem((n_angle, NG // 2, LANES), F32),
            vmem((n_angle, NG // 2, LANES), F32),
            vmem((n_angle, 64, width), BF16),
            vmem((16, NG * NG), F32),
            dma((5,)), dma((3,)), dma((2,)), dma((2,)), dma((2,)), dma((2,)),
            dma((n_angle,)), dma((n_angle,)), dma((n_strip,)), dma((n_strip,)),
            dma((n_angle,)), dma((n_angle,)), dma((n_strip,)), dma((n_strip,)),
        ],
        compiler_params=pltpu.CompilerParams(
            collective_id=0, has_side_effects=True, vmem_limit_bytes=48 * 1024 * 1024
        ),
        name="gradient_step",
    )(
        cols, trig, object_field[:, 0], amplitudes[0], probe_field, fwd, inv
    )
    return (
        object_grad[:, None],
        probe_grad.reshape(2, FRAME, FRAME),
        volume[None, None],
    )


def solution(mesh):
    return jax.shard_map(
        shards,
        mesh=mesh,
        in_specs=(
            P(None, "angle", "strip", None),
            P("angle", "strip", None, None),
            P("angle", "strip", None),
            P(),
            P(),
        ),
        out_specs=(P(None, "angle", "strip", None), P(), P("strip", "angle", None, None)),
        check_vma=False,
    )
```

time: 1390 us -> 84.2 us (0.06)
  the two profiles are of different devices: /device:TPU:1 before, /device:TPU:0 now
where the time goes in v1:
time: 84.2 us; the launch traced here: 83.8 us
  Pallas kernels  73.1 us (87%)
  local copies, waits for them, and re-layouts  10.1 us (12%)
    pallas_call x1, Pallas kernels, shards(): pl.pallas_call(lambda *refs: kernel(n_angle, n_strip, scale, *refs), out_...  73.1 us
    unnamed x15, local copies, waits for them, and re-layouts  8.77 us

profile of v1, /device:TPU:0, one launch (start us, length us, event | category | flops | bytes accessed | tf_op | source)
XLA Modules:
  0.0 83.8 jit_solution(17412504203129927837)
XLA Ops:
  0.6 1.3 %slice.3 = s32[1,1,1]{1,2,0:T(1,128)} slice(s32[1,4,2]{1,2,0:T(2,128)} %param.9), slice={[0:1], [3:4], [1:2]} | slice | bytes 8 | tf_op jit(solution)/shard_map/slice | solution.py:420
  1.9 0.0 copy-start.5
  1.9 0.7 copy-done.5
  2.6 0.0 copy-start
  2.6 1.2 %copy-done = f32[2,1,128,1024]{3,2,1,0:T(8,128)S(1)} copy-done((f32[2,1,128,1024]{3,2,1,0:T(8,128)S(1)}, f32[2,1,128,1024]{3,2,1,0:T(8,128)}, u32[]{:S(2)}) %copy-start) | copy-done | bytes 1048600
  3.8 0.0 copy-start.1
  3.8 1.0 %copy-done.1 = bf16[1,4,256,256]{3,2,1,0:T(8,128)(2,1)S(1)} copy-done((bf16[1,4,256,256]{3,2,1,0:T(8,128)(2,1)S(1)}, bf16[1,4,256,256]{3,2,1,0:T(8,128)(2,1)}, u32[]{:S(2)}) %copy-start.1) | copy-done | bytes 524312
  4.9 0.0 copy-start.2
  4.9 1.0 %copy-done.2 = f32[2,256,256]{2,1,0:T(8,128)S(1)} copy-done((f32[2,256,256]{2,1,0:T(8,128)S(1)}, f32[2,256,256]{2,1,0:T(8,128)}, u32[]{:S(2)}) %copy-start.2) | copy-done | bytes 524312
  5.9 0.0 copy-start.3
  5.9 1.0 %copy-done.3 = bf16[512,512]{1,0:T(8,128)(2,1)S(1)} copy-done((bf16[512,512]{1,0:T(8,128)(2,1)S(1)}, bf16[512,512]{1,0:T(8,128)(2,1)}, u32[]{:S(2)}) %copy-start.3) | copy-done | bytes 524312
  7.0 0.0 copy-start.4
  7.0 1.0 %copy-done.4 = bf16[512,512]{1,0:T(8,128)(2,1)S(1)} copy-done((bf16[512,512]{1,0:T(8,128)(2,1)S(1)}, bf16[512,512]{1,0:T(8,128)(2,1)}, u32[]{:S(2)}) %copy-start.4) | copy-done | bytes 524312
  8.0 73.1 %gradient_step.1 = (f32[2,128,1024]{2,1,0:T(8,128)S(1)}, f32[512,256]{1,0:T(8,128)S(1)}, f32[16,16384]{1,0:T(8,128)S(1)}) custom-call(s32[1]{0:T(128)} %bitcast.refs_0_, f32[2,8]{1,0:T(2,128)S(1)} %pad_maximum_fusion.refs_1_, f32[2,128,1024]{2,1,0:T(8,128)S(1)} %bitcast.12, bf16[4,256,256]{2,1,0:T(8,128)(2,1)S(1)} %bitcast.15, f32[2,256,256]{2,1,0:T(8,128)S(1)} %copy-done.2, ...), custom_call_target="tpu_custom_call" | custom-call | tf_op jit(solution)/shard_map/gradient_step/pallas_call | solution.py:425
  81.1 1.0 %copy.14 = f32[2,1,128,1024]{3,2,1,0:T(8,128)} copy(f32[2,1,128,1024]{3,2,1,0:T(8,128)S(1)} %bitcast.14) | data formatting | bytes 2097152
  82.1 0.8 copy.15
  82.9 1.0 %copy.16 = f32[1,1,16,16384]{3,2,1,0:T(8,128)} copy(f32[1,1,16,16384]{3,2,1,0:T(8,128)S(1)} %bitcast.13) | data formatting | bytes 2097152
  (2 shorter events, 0.1 us)
Async XLA Ops:
  1.9 0.7 copy-start.5
  2.6 1.2 %copy-start = (f32[2,1,128,1024]{3,2,1,0:T(8,128)S(1)}, f32[2,1,128,1024]{3,2,1,0:T(8,128)}, u32[]{:S(2)}) copy-start(f32[2,1,128,1024]{3,2,1,0:T(8,128)} %param.7) | copy-start | bytes 3145732
  3.8 1.0 %copy-start.1 = (bf16[1,4,256,256]{3,2,1,0:T(8,128)(2,1)S(1)}, bf16[1,4,256,256]{3,2,1,0:T(8,128)(2,1)}, u32[]{:S(2)}) copy-start(bf16[1,4,256,256]{3,2,1,0:T(8,128)(2,1)} %param.8) | copy-start | bytes 1572868
  4.9 1.0 %copy-start.2 = (f32[2,256,256]{2,1,0:T(8,128)S(1)}, f32[2,256,256]{2,1,0:T(8,128)}, u32[]{:S(2)}) copy-start(f32[2,256,256]{2,1,0:T(8,128)} %refs_4_.1) | copy-start | bytes 1572868
  5.9 1.0 %copy-start.3 = (bf16[512,512]{1,0:T(8,128)(2,1)S(1)}, bf16[512,512]{1,0:T(8,128)(2,1)}, u32[]{:S(2)}) copy-start(bf16[512,512]{1,0:T(8,128)(2,1)} %constant.5.clone.refs_6_) | copy-start | bytes 1572868
  7.0 1.0 %copy-start.4 = (bf16[512,512]{1,0:T(8,128)(2,1)S(1)}, bf16[512,512]{1,0:T(8,128)(2,1)}, u32[]{:S(2)}) copy-start(bf16[512,512]{1,0:T(8,128)(2,1)} %constant.4.clone.refs_5_) | copy-start | bytes 1572868

commit v2 on v1

--- a/solution.py
+++ b/solution.py
@@ -16,7 +16,7 @@
 F32 = jnp.float32
 BF16 = jnp.bfloat16
 FIXED_COLS = (768, 0, 384)
-WINDOW = (256, 768)
+WINDOW = (320, 704)
 
 
 def dft_blocks():
@@ -31,7 +31,7 @@
 
 def kernel(
     n_angle, n_strip, scale,
-    cols, trig, obj_hbm, amp_hbm, probe_hbm, fwd_hbm, inv_hbm,
+    offs, trig, obj_hbm, amp_hbm, probe_hbm, fwd_hbm, inv_hbm,
     og_hbm, pg_hbm, vol_hbm,
     ext, probe, amp, fwd, inv,
     halo_out, halo_in, place_t, place_m, moved3, patch3, xbuf, ybuf, wbuf, mbuf, zbuf, gbuf,
@@ -39,13 +39,15 @@
     pterm, rs_in, ar_in, ag_in, pg_out,
     lower_t, frac_t, lhs, vol,
     load_sem, store_sem, halo_s, halo_r, grad_s, grad_r, a2a_s, a2a_r,
-    rs_s, rs_r, ar_s, ar_r, ag_s, ag_r,
+    rs_s, rs_r, ar_s, ar_r, ag_s, ag_r, mate_s, mate_r, part_s, part_r,
 ):
     width = ext.shape[2]
     me_a = lax.axis_index("angle")
     me_s = lax.axis_index("strip")
     above = lax.rem(me_s + n_strip - 1, n_strip)
     below = lax.rem(me_s + 1, n_strip)
+    core_at = lax.rem(me_s, 2)
+    mate = me_s + 1 - 2 * core_at
 
     loads = [
         pltpu.make_async_copy(obj_hbm, ext.at[:, pl.ds(HALO, 128), :], load_sem.at[0]),
@@ -97,7 +99,7 @@
     for copy in halo_copies:
         copy.start()
 
-    col = cols[0].astype(F32)
+    col = offs[0, 1, 3].astype(F32)
     for b in range(width // LANES):
         at = lax.broadcasted_iota(jnp.int32, (LANES, FRAME), 0) + b * LANES
         of = lax.broadcasted_iota(jnp.int32, (LANES, FRAME), 1)
@@ -151,15 +153,17 @@
     exit_chunk(2)
 
     center = (NG - 1) / 2.0
-    half_x = NG // 2
-    xpos = lax.broadcasted_iota(jnp.int32, (half_x, LANES), 0).astype(F32) - center
-    ypos = lax.broadcasted_iota(jnp.int32, (half_x, LANES), 1).astype(F32) - center
+    n_rows = NG // 4
+    first_row = core_at * n_rows
+    shape = (n_rows, LANES)
+    xpos = (lax.broadcasted_iota(jnp.int32, shape, 0) + first_row).astype(F32) - center
+    ypos = lax.broadcasted_iota(jnp.int32, shape, 1).astype(F32) - center
 
     @pl.loop(0, n_angle)
     def _(a):
         upos = (width - 1) / 2.0 + 2.0 * (xpos * trig[0, a] + ypos * trig[1, a])
         low = jnp.clip(jnp.floor(upos), 0.0, width - 2.0)
-        lower_t[a] = low
+        lower_t[a] = low - float(WINDOW[0])
         frac_t[a] = upos - low
 
     for copy in halo_copies:
@@ -191,7 +195,7 @@
             row = pl.multiple_of(step * 16, 16)
             wr, wi = wbuf[pl.ds(row, 16), :], wbuf[pl.ds(FRAME + row, 16), :]
             measured = amp[f, pl.ds(row, 16), :].astype(F32)
-            factor = 1.0 - measured / jnp.sqrt(wr * wr + wi * wi + 1.0)
+            factor = 1.0 - measured * lax.rsqrt(wr * wr + wi * wi + 1.0)
             mbuf[f, pl.ds(row, 16), :] = (wr * factor).astype(BF16)
             mbuf[f, pl.ds(FRAME + row, 16), :] = (wi * factor).astype(BF16)
 
@@ -267,10 +271,7 @@
             rs_s.at[d], rs_r.at[d], strip=peer,
         )
 
-    @pl.loop(1, n_strip)
-    def _(d):
-        rs_copy(d).start()
-
+    around = (WINDOW[0] // LANES * LANES, -(-WINDOW[1] // LANES) * LANES)
     for copy in grad_copies:
         copy.wait()
     for side, present in ((0, has_above), (1, has_below)):
@@ -287,22 +288,40 @@
             core[0, rows, :] = got[0]
             core[1, rows, :] = got[1]
             own = pl.ds(HALO + side * HALO + local, 16)
-            phase[rows, :] = (ext[0, own, :] * got[1] - ext[1, own, :] * got[0]).astype(BF16)
+            cut = slice(around[0], around[1])
+            value = ext[0, own, cut] * got[1][:, cut] - ext[1, own, cut] * got[0][:, cut]
+            value = pltpu.roll(value, around[1] - WINDOW[0], 1)
+            phase[rows, :] = value[:, : WINDOW[1] - WINDOW[0]].astype(BF16)
 
     def a2a_copy(d):
         peer = lax.rem(me_a + d, n_angle)
         return remote(
-            phase.at[pl.ds(pl.multiple_of(peer * 16, 16), 16)], ph_all.at[me_a],
+            phase.at[pl.ds(pl.multiple_of(peer * 16, 16), 16)], ph_all.at[core_at, me_a],
             a2a_s.at[d], a2a_r.at[d], angle=peer,
         )
 
+    def mate_copy(d):
+        at = ph_all.at[core_at, lax.rem(me_a + n_angle - d, n_angle)]
+        return remote(at, at, mate_s.at[d], mate_r.at[d], strip=mate)
+
     @pl.loop(1, n_angle)
     def _(d):
         a2a_copy(d).start()
+
+    ph_all[core_at, me_a] = phase[pl.ds(pl.multiple_of(me_a * 16, 16), 16), :]
+    mate_copy(0).start()
+
+    @pl.loop(1, n_strip)
+    def _(d):
+        rs_copy(d).start()
 
     store_og = pltpu.make_async_copy(core, og_hbm, store_sem.at[0])
     store_og.start()
-    ph_all[me_a] = phase[pl.ds(pl.multiple_of(me_a * 16, 16), 16), :]
+
+    @pl.loop(1, n_angle)
+    def _(d):
+        a2a_copy(d).wait()
+        mate_copy(d).start()
 
     @pl.loop(1, n_strip)
     def _(d):
@@ -323,53 +342,82 @@
     def _(d):
         ar_copy(d).start()
 
-    @pl.loop(1, n_angle)
-    def _(d):
-        a2a_copy(d).wait()
+    @pl.loop(0, n_angle)
+    def _(d):
+        mate_copy(d).wait()
 
     flip = (
         lax.broadcasted_iota(jnp.int32, (LANES, LANES), 0)
         + lax.broadcasted_iota(jnp.int32, (LANES, LANES), 1)
         == LANES - 1
     ).astype(F32).astype(BF16)
+    n_cols = WINDOW[1] - WINDOW[0]
 
     @pl.loop(0, n_angle)
     def _(a):
-        rows = ph_all[a]
+        rows = jnp.concatenate([ph_all[0, a], ph_all[1, a]], axis=0)
         mirrored = [
-            jnp.dot(rows[:, b * LANES : (b + 1) * LANES], flip, preferred_element_type=F32)
-            for b in range(8)
+            jnp.dot(rows[:, b : b + LANES], flip, preferred_element_type=F32)
+            for b in range(0, n_cols, LANES)
         ]
         both = jnp.concatenate(
             [rows.astype(F32), jnp.concatenate(mirrored[::-1], axis=1)], axis=0
         )
-        lhs[a, :32, :] = both.astype(BF16)
-        lhs[a, 32:, :] = pltpu.roll(both, width - 1, 1).astype(BF16)
+        lhs[a, :64, :] = both.astype(BF16)
+        lhs[a, 64:, :] = pltpu.roll(both, n_cols - 1, 1).astype(BF16)
 
     column = lax.broadcasted_iota(jnp.int32, (LANES, LANES), 0).astype(F32).astype(BF16)
     one, zero = jnp.ones((), BF16), jnp.zeros((), BF16)
 
-    def project(x):
-        total = jnp.zeros((32, LANES), F32)
+    def one_hot(a, i):
+        low = lower_t[a, pl.ds(i, 1), :]
+        return jnp.concatenate(
+            [
+                jnp.where(column == (low - float(j)).astype(BF16), one, zero)
+                for j in range(0, n_cols, LANES)
+            ],
+            axis=0,
+        )
+
+    def project(pair):
+        totals = [jnp.zeros((64, LANES), F32) for _ in range(2)]
         for a in range(n_angle):
-            low = lower_t[a, pl.ds(x, 1), :] - float(WINDOW[0])
-            frac = frac_t[a, pl.ds(x, 1), :]
-            picks = jnp.concatenate(
-                [
-                    jnp.where(column == (low - float(j * LANES)).astype(BF16), one, zero)
-                    for j in range((WINDOW[1] - WINDOW[0]) // LANES)
-                ],
-                axis=0,
+            picks = jnp.concatenate([one_hot(a, 2 * pair + k) for k in range(2)], axis=1)
+            got = jnp.dot(lhs[a], picks, preferred_element_type=F32)
+            for k in range(2):
+                frac = frac_t[a, pl.ds(2 * pair + k, 1), :]
+                part = got[:, k * LANES : (k + 1) * LANES]
+                totals[k] = totals[k] + (part[:64] * (1.0 - frac) + part[64:] * frac)
+        for k in range(2):
+            x = first_row + 2 * pair + k
+            turned = joined(
+                jnp.dot(split(totals[k][32:]), flip, preferred_element_type=F32)
             )
-            got = jnp.dot(lhs[a, :, WINDOW[0] : WINDOW[1]], picks, preferred_element_type=F32)
-            total = total + (got[:32] * (1.0 - frac) + got[32:] * frac)
-        vol[:, pl.ds(pl.multiple_of(x * LANES, LANES), LANES)] = total[:16]
-        high = total[16:].astype(BF16)
-        rest = (total[16:] - high.astype(F32)).astype(BF16)
-        turned = jnp.dot(jnp.concatenate([high, rest], axis=0), flip, preferred_element_type=F32)
-        vol[:, pl.ds(pl.multiple_of((NG - 1 - x) * LANES, LANES), LANES)] = turned[:16] + turned[16:]
-
-    pl.loop(0, half_x // 2)(project)
+            here = pl.ds(pl.multiple_of(x * LANES, LANES), LANES)
+            there = pl.ds(pl.multiple_of((NG - 1 - x) * LANES, LANES), LANES)
+            for c in range(2):
+                vol[c, :, here] = totals[k][c * 16 : c * 16 + 16]
+                vol[c, :, there] = turned[c * 16 : c * 16 + 16]
+
+    part_cols = n_rows // 2 * LANES
+
+    def part_at(owner, half, side):
+        row = owner * n_rows + half * (n_rows // 2)
+        if side:
+            row = NG - row - n_rows // 2
+        return pl.ds(pl.multiple_of(row * LANES, LANES), part_cols)
+
+    def part_copy(half, side):
+        at = vol.at[1 - core_at, :, part_at(core_at, half, side)]
+        return remote(at, at, part_s.at[half, side], part_r.at[half, side], strip=mate)
+
+    def part_arrived(half, side):
+        at = vol.at[core_at, :, part_at(1 - core_at, half, side)]
+        return remote(at, at, part_s.at[half, side], part_r.at[half, side], strip=mate)
+
+    pl.loop(0, n_rows // 4)(project)
+    for side in range(2):
+        part_copy(0, side).start()
 
     @pl.loop(1, n_angle)
     def _(d):
@@ -390,9 +438,9 @@
     def _(d):
         ag_copy(d).start()
 
-    pl.loop(half_x // 2, half_x)(project)
-    store_vol = pltpu.make_async_copy(vol, vol_hbm, store_sem.at[1])
-    store_vol.start()
+    pl.loop(n_rows // 4, n_rows // 2)(project)
+    for side in range(2):
+        part_copy(1, side).start()
 
     def ag_arrived(d):
         sender = lax.rem(me_s + n_strip - d, n_strip)
@@ -407,9 +455,15 @@
     pg_out[...] = ag_in[...].astype(F32)
     store_pg = pltpu.make_async_copy(pg_out, pg_hbm, store_sem.at[2])
     store_pg.start()
+    for half in range(2):
+        for side in range(2):
+            part_copy(half, side).wait_send()
+            part_arrived(half, side).wait_recv()
+    store_vol = pltpu.make_async_copy(vol.at[core_at], vol_hbm, store_sem.at[1])
+    store_vol.start()
     store_og.wait()
+    store_pg.wait()
     store_vol.wait()
-    store_pg.wait()
 
 
 def shards(object_field, amplitudes, scan_offsets, probe_field, tilt_angles):
@@ -417,9 +471,9 @@
     width = object_field.shape[3]
     fwd, inv = dft_blocks()
     trig = jnp.stack([jnp.cos(tilt_angles), jnp.sin(tilt_angles)])
-    cols = scan_offsets[0, 3:, 1]
     scale = 1.0 / math.sqrt(n_angle * n_strip * scan_offsets.shape[1])
-    hbm = pl.BlockSpec(memory_space=pl.ANY)
+    n_cols = WINDOW[1] - WINDOW[0]
+    hbm = pl.BlockSpec(memory_space=pltpu.HBM)
     smem = pl.BlockSpec(memory_space=pltpu.SMEM)
     vmem, dma = pltpu.VMEM, pltpu.SemaphoreType.DMA
     object_grad, probe_grad, volume = pl.pallas_call(
@@ -452,27 +506,28 @@
             vmem((2, 2, HALO, width), BF16),
             vmem((2, 2, HALO, width), BF16),
             vmem((2, 128, width), F32),
-            vmem((128, width), BF16),
-            vmem((n_angle, 16, width), BF16),
+            vmem((128, n_cols), BF16),
+            vmem((2, n_angle, 16, n_cols), BF16),
             vmem((2 * FRAME, FRAME), BF16),
             vmem((n_strip, 16, FRAME), BF16),
             vmem((n_angle, 16, FRAME), F32),
             vmem((2 * FRAME, FRAME), BF16),
             vmem((2 * FRAME, FRAME), F32),
-            vmem((n_angle, NG // 2, LANES), F32),
-            vmem((n_angle, NG // 2, LANES), F32),
-            vmem((n_angle, 64, width), BF16),
-            vmem((16, NG * NG), F32),
+            vmem((n_angle, NG // 4, LANES), F32),
+            vmem((n_angle, NG // 4, LANES), F32),
+            vmem((n_angle, 128, n_cols), BF16),
+            vmem((2, 16, NG * NG), F32),
             dma((5,)), dma((3,)), dma((2,)), dma((2,)), dma((2,)), dma((2,)),
             dma((n_angle,)), dma((n_angle,)), dma((n_strip,)), dma((n_strip,)),
             dma((n_angle,)), dma((n_angle,)), dma((n_strip,)), dma((n_strip,)),
+            dma((n_angle,)), dma((n_angle,)), dma((2, 2)), dma((2, 2)),
         ],
         compiler_params=pltpu.CompilerParams(
-            collective_id=0, has_side_effects=True, vmem_limit_bytes=48 * 1024 * 1024
+            collective_id=0, has_side_effects=True, vmem_limit_bytes=60 * 1024 * 1024
         ),
         name="gradient_step",
     )(
-        cols, trig, object_field[:, 0], amplitudes[0], probe_field, fwd, inv
+        scan_offsets.transpose(0, 2, 1), trig, object_field[:, 0], amplitudes[0], probe_field, fwd, inv
     )
     return (
         object_grad[:, None],

time: 84.2 us -> 61.3 us (0.73)
  the two profiles are of different devices: /device:TPU:0 before, /device:TPU:1 now
where the time goes in v2:
time: 61.3 us; the launch traced here: 61.2 us
  Pallas kernels  55 us (90%)
  local copies, waits for them, and re-layouts  4.88 us (8%)
  between operations  0.67 us (1%)
    pallas_call x1, Pallas kernels, shards(): pl.pallas_call(lambda *refs: kernel(n_angle, n_strip, scale, *refs), out_...  55 us
    unnamed x9, local copies, waits for them, and re-layouts  4.84 us

profile of v2, /device:TPU:1, one launch (start us, length us, event | category | flops | bytes accessed | tf_op | source)
XLA Modules:
  0.0 61.2 jit_solution(14358203977029870699)
XLA Ops:
  0.6 0.0 copy-start.2
  0.6 0.6 %copy-done.2 = f32[8]{0:T(128)S(1)} copy-done((f32[8]{0:T(128)S(1)}, f32[8]{0:T(128)}, u32[]{:S(2)}) %copy-start.2) | copy-done | bytes 56
  1.3 0.6 pad_maximum_fusion.refs_1_
  1.9 55.0 %gradient_step.1 = (f32[2,128,1024]{2,1,0:T(8,128)}, f32[512,256]{1,0:T(8,128)}, f32[16,16384]{1,0:T(8,128)}) custom-call(s32[1,2,4]{2,1,0:T(2,128)} %bitcast.17, f32[2,8]{1,0:T(2,128)} %pad_maximum_fusion.refs_1_, f32[2,128,1024]{2,1,0:T(8,128)} %bitcast.14, bf16[4,256,256]{2,1,0:T(8,128)(2,1)} %bitcast.16, f32[2,256,256]{2,1,0:T(8,128)} %refs_4_.1, ...), custom_call_target="tpu_custom_call" | custom-call | tf_op jit(solution)/shard_map/gradient_step/pallas_call | solution.py:479
  56.9 0.0 copy-start.1
  57.0 0.0 copy-start
  57.0 2.4 %copy.14 = f32[2,1,128,1024]{3,2,1,0:T(8,128)} copy(f32[2,1,128,1024]{3,2,1,0:T(8,128)} %bitcast.13) | data formatting | bytes 2097152
  59.4 0.0 copy-done.1
  59.4 0.8 %copy.15 = f32[2,256,256]{2,1,0:T(8,128)} copy(f32[2,256,256]{2,1,0:T(8,128)S(1)} %bitcast.15) | data formatting | bytes 1048576
  60.2 0.0 copy-done
  60.2 1.0 %copy.16 = f32[1,1,16,16384]{3,2,1,0:T(8,128)} copy(f32[1,1,16,16384]{3,2,1,0:T(8,128)S(1)} %bitcast.12) | data formatting | bytes 2097152
  (1 shorter events, 0.0 us)
Async XLA Ops:
  0.6 0.7 %copy-start.2 = (f32[8]{0:T(128)S(1)}, f32[8]{0:T(128)}, u32[]{:S(2)}) copy-start(f32[8]{0:T(128)} %param.11) | copy-start | bytes 100
  56.9 2.4 %copy-start.1 = (f32[512,256]{1,0:T(8,128)S(1)}, f32[512,256]{1,0:T(8,128)}, u32[]{:S(2)}) copy-start(f32[512,256]{1,0:T(8,128)} %get-tuple-element.7) | copy-start | bytes 1572868
  57.0 3.2 %copy-start = (f32[16,16384]{1,0:T(8,128)S(1)}, f32[16,16384]{1,0:T(8,128)}, u32[]{:S(2)}) copy-start(f32[16,16384]{1,0:T(8,128)} %get-tuple-element.8) | copy-start | bytes 3145732

commit v3 on v2

--- a/solution.py
+++ b/solution.py
@@ -37,9 +37,9 @@
     halo_out, halo_in, place_t, place_m, moved3, patch3, xbuf, ybuf, wbuf, mbuf, zbuf, gbuf,
     grad_out, grad_in, core, phase, ph_all,
     pterm, rs_in, ar_in, ag_in, pg_out,
-    lower_t, frac_t, lhs, vol,
+    lower_t, frac_t, lhs, total, vol,
     load_sem, store_sem, halo_s, halo_r, grad_s, grad_r, a2a_s, a2a_r,
-    rs_s, rs_r, ar_s, ar_r, ag_s, ag_r, mate_s, mate_r, part_s, part_r,
+    rs_s, rs_r, ar_s, ar_r, ag_s, ag_r, mate_s, mate_r, part_s, part_r, own_sem, mate_sem,
 ):
     width = ext.shape[2]
     me_a = lax.axis_index("angle")
@@ -164,6 +164,9 @@
         upos = (width - 1) / 2.0 + 2.0 * (xpos * trig[0, a] + ypos * trig[1, a])
         low = jnp.clip(jnp.floor(upos), 0.0, width - 2.0)
         lower_t[a] = low - float(WINDOW[0])
+        total[pl.ds(a * (n_rows // n_angle), n_rows // n_angle)] = jnp.zeros(
+            (n_rows // n_angle, 64, LANES), F32
+        )
         frac_t[a] = upos - low
 
     for copy in halo_copies:
@@ -186,25 +189,23 @@
     loads[3].wait()
     loads[4].wait()
 
-    @pl.loop(0, 4)
-    def _(f):
-        wbuf[...] = jnp.dot(fwd[...], ybuf[f], preferred_element_type=F32)
-
-        @pl.loop(0, FRAME // 16)
-        def _(step):
-            row = pl.multiple_of(step * 16, 16)
-            wr, wi = wbuf[pl.ds(row, 16), :], wbuf[pl.ds(FRAME + row, 16), :]
-            measured = amp[f, pl.ds(row, 16), :].astype(F32)
-            factor = 1.0 - measured * lax.rsqrt(wr * wr + wi * wi + 1.0)
-            mbuf[f, pl.ds(row, 16), :] = (wr * factor).astype(BF16)
-            mbuf[f, pl.ds(FRAME + row, 16), :] = (wi * factor).astype(BF16)
-
+    def misfit(f, rows):
+        wr, wi = wbuf[f, rows, :], wbuf[f, rows.start + FRAME : rows.stop + FRAME, :]
+        measured = amp[f, rows, :].astype(F32)
+        factor = 1.0 - measured * lax.rsqrt(wr * wr + wi * wi + 1.0)
+        mbuf[f, rows, :] = (wr * factor).astype(BF16)
+        mbuf[f, rows.start + FRAME : rows.stop + FRAME, :] = (wi * factor).astype(BF16)
+
+    for f in range(4):
+        wbuf[f] = jnp.dot(fwd[...], ybuf[f], preferred_element_type=F32)
+        for row in range(0, FRAME, 32):
+            misfit(f, slice(row, row + 32))
+    for f in range(4):
         back = jnp.dot(inv[...], mbuf[f], preferred_element_type=F32).astype(BF16)
         for chunk in range(4):
             at = chunk * HALO
-            rows = pl.ds(pl.multiple_of(f * HALO, HALO), HALO)
-            zbuf[chunk, rows, :FRAME] = back[at : at + HALO]
-            zbuf[chunk, rows, FRAME:] = back[FRAME + at : FRAME + at + HALO]
+            zbuf[chunk, f * HALO : (f + 1) * HALO, :FRAME] = back[at : at + HALO]
+            zbuf[chunk, f * HALO : (f + 1) * HALO, FRAME:] = back[FRAME + at : FRAME + at + HALO]
 
     def place(terms, moved):
         blocks = [moved[:, b * LANES : (b + 1) * LANES] for b in range(width // LANES)]
@@ -271,6 +272,10 @@
             rs_s.at[d], rs_r.at[d], strip=peer,
         )
 
+    @pl.loop(1, n_strip)
+    def _(d):
+        rs_copy(d).start()
+
     around = (WINDOW[0] // LANES * LANES, -(-WINDOW[1] // LANES) * LANES)
     for copy in grad_copies:
         copy.wait()
@@ -293,6 +298,10 @@
             value = pltpu.roll(value, around[1] - WINDOW[0], 1)
             phase[rows, :] = value[:, : WINDOW[1] - WINDOW[0]].astype(BF16)
 
+    def farness(step):
+        near = (step + 1) // 2
+        return jnp.where(lax.rem(step, 2) == 1, near, lax.rem(n_angle - near, n_angle))
+
     def a2a_copy(d):
         peer = lax.rem(me_a + d, n_angle)
         return remote(
@@ -300,28 +309,24 @@
             a2a_s.at[d], a2a_r.at[d], angle=peer,
         )
 
-    def mate_copy(d):
-        at = ph_all.at[core_at, lax.rem(me_a + n_angle - d, n_angle)]
-        return remote(at, at, mate_s.at[d], mate_r.at[d], strip=mate)
-
-    @pl.loop(1, n_angle)
-    def _(d):
+    def cross_copy(d):
+        peer = lax.rem(me_a + d, n_angle)
+        return remote(
+            phase.at[pl.ds(pl.multiple_of(peer * 16, 16), 16)], ph_all.at[core_at, me_a],
+            mate_s.at[d], mate_r.at[d], angle=peer, strip=mate,
+        )
+
+    @pl.loop(0, n_angle - 1)
+    def _(step):
+        d = farness(n_angle - 1 - step)
         a2a_copy(d).start()
-
+        cross_copy(d).start()
+
+    cross_copy(0).start()
     ph_all[core_at, me_a] = phase[pl.ds(pl.multiple_of(me_a * 16, 16), 16), :]
-    mate_copy(0).start()
-
-    @pl.loop(1, n_strip)
-    def _(d):
-        rs_copy(d).start()
 
     store_og = pltpu.make_async_copy(core, og_hbm, store_sem.at[0])
     store_og.start()
-
-    @pl.loop(1, n_angle)
-    def _(d):
-        a2a_copy(d).wait()
-        mate_copy(d).start()
 
     @pl.loop(1, n_strip)
     def _(d):
@@ -330,7 +335,7 @@
     own_rows = pl.ds(pl.multiple_of(me_s * 16, 16), 16)
     ar_in[me_a] = lax.fori_loop(
         1, n_strip, lambda d, acc: acc + rs_in[d].astype(F32), pterm[own_rows, :].astype(F32)
-    )
+    ).astype(BF16)
 
     def ar_copy(d):
         peer = lax.rem(me_a + d, n_angle)
@@ -341,10 +346,6 @@
     @pl.loop(1, n_angle)
     def _(d):
         ar_copy(d).start()
-
-    @pl.loop(0, n_angle)
-    def _(d):
-        mate_copy(d).wait()
 
     flip = (
         lax.broadcasted_iota(jnp.int32, (LANES, LANES), 0)
@@ -352,22 +353,28 @@
         == LANES - 1
     ).astype(F32).astype(BF16)
     n_cols = WINDOW[1] - WINDOW[0]
-
-    @pl.loop(0, n_angle)
-    def _(a):
-        rows = jnp.concatenate([ph_all[0, a], ph_all[1, a]], axis=0)
-        mirrored = [
-            jnp.dot(rows[:, b : b + LANES], flip, preferred_element_type=F32)
-            for b in range(0, n_cols, LANES)
-        ]
-        both = jnp.concatenate(
-            [rows.astype(F32), jnp.concatenate(mirrored[::-1], axis=1)], axis=0
-        )
-        lhs[a, :64, :] = both.astype(BF16)
-        lhs[a, 64:, :] = pltpu.roll(both, n_cols - 1, 1).astype(BF16)
-
     column = lax.broadcasted_iota(jnp.int32, (LANES, LANES), 0).astype(F32).astype(BF16)
     one, zero = jnp.ones((), BF16), jnp.zeros((), BF16)
+
+    def ag_copy(d):
+        peer = lax.rem(me_s + d, n_strip)
+        return remote(
+            ag_in.at[own_rows], ag_in.at[own_rows], ag_s.at[d], ag_r.at[d], strip=peer
+        )
+
+    def gather_probe():
+        @pl.loop(1, n_angle)
+        def _(d):
+            ar_copy(d).wait()
+
+        summed = ar_in[0].astype(F32)
+        for a in range(1, n_angle):
+            summed = summed + ar_in[a].astype(F32)
+        ag_in[own_rows, :] = (summed * scale).astype(BF16)
+
+        @pl.loop(1, n_strip)
+        def _(d):
+            ag_copy(d).start()
 
     def one_hot(a, i):
         low = lower_t[a, pl.ds(i, 1), :]
@@ -379,68 +386,79 @@
             axis=0,
         )
 
-    def project(pair):
-        totals = [jnp.zeros((64, LANES), F32) for _ in range(2)]
-        for a in range(n_angle):
-            picks = jnp.concatenate([one_hot(a, 2 * pair + k) for k in range(2)], axis=1)
-            got = jnp.dot(lhs[a], picks, preferred_element_type=F32)
-            for k in range(2):
-                frac = frac_t[a, pl.ds(2 * pair + k, 1), :]
-                part = got[:, k * LANES : (k + 1) * LANES]
-                totals[k] = totals[k] + (part[:64] * (1.0 - frac) + part[64:] * frac)
+    def project(a, pair):
+        picks = jnp.concatenate([one_hot(a, 2 * pair + k) for k in range(2)], axis=1)
+        got = jnp.dot(lhs[...], picks, preferred_element_type=F32)
         for k in range(2):
-            x = first_row + 2 * pair + k
-            turned = joined(
-                jnp.dot(split(totals[k][32:]), flip, preferred_element_type=F32)
-            )
+            frac = frac_t[a, pl.ds(2 * pair + k, 1), :]
+            part = got[:, k * LANES : (k + 1) * LANES]
+            total[2 * pair + k] += part[:64] * (1.0 - frac) + part[64:] * frac
+
+    @pl.loop(0, n_angle)
+    def _(step):
+        d = farness(step)
+        a = lax.rem(me_a + n_angle - d, n_angle)
+
+        @pl.when(step > 0)
+        def _():
+            a2a_copy(d).wait()
+
+        cross_copy(d).wait()
+        rows = jnp.concatenate([ph_all[0, a], ph_all[1, a]], axis=0)
+        mirrored = [
+            jnp.dot(rows[:, b : b + LANES], flip, preferred_element_type=F32)
+            for b in range(0, n_cols, LANES)
+        ]
+        both = jnp.concatenate(
+            [rows.astype(F32), jnp.concatenate(mirrored[::-1], axis=1)], axis=0
+        )
+        lhs[:64, :] = both.astype(BF16)
+        lhs[64:, :] = pltpu.roll(both, n_cols - 1, 1).astype(BF16)
+
+        @pl.loop(0, n_rows // 16)
+        def _(group):
+            for pair in range(8):
+                project(a, group * 8 + pair)
+
+        @pl.when(step == n_angle - 2)
+        def _():
+            gather_probe()
+
+    n_groups = n_rows // 8
+    group_cols = 8 * LANES
+
+    def group_at(owner, group, side):
+        row = owner * n_rows + group * 8
+        if side:
+            row = NG - row - 8
+        return pl.ds(pl.multiple_of(row * LANES, LANES), group_cols)
+
+    def part_copy(group, side):
+        at = vol.at[1 - core_at, :, group_at(core_at, group, side)]
+        return remote(at, at, part_s.at[group, side], part_r.at[group, side], strip=mate)
+
+    def part_arrived(group, side):
+        at = vol.at[core_at, :, group_at(1 - core_at, group, side)]
+        return remote(at, at, part_s.at[group, side], part_r.at[group, side], strip=mate)
+
+    def store_part(owner, group, side, sem):
+        cols = group_at(owner, group, side)
+        return pltpu.make_async_copy(vol.at[core_at, :, cols], vol_hbm.at[:, cols], sem)
+
+    @pl.loop(0, n_groups)
+    def _(group):
+        stack = jnp.concatenate([total[group * 8 + k, 32:] for k in range(8)], axis=0)
+        turned = joined(jnp.dot(split(stack), flip, preferred_element_type=F32))
+        for k in range(8):
+            x = first_row + group * 8 + k
             here = pl.ds(pl.multiple_of(x * LANES, LANES), LANES)
             there = pl.ds(pl.multiple_of((NG - 1 - x) * LANES, LANES), LANES)
             for c in range(2):
-                vol[c, :, here] = totals[k][c * 16 : c * 16 + 16]
-                vol[c, :, there] = turned[c * 16 : c * 16 + 16]
-
-    part_cols = n_rows // 2 * LANES
-
-    def part_at(owner, half, side):
-        row = owner * n_rows + half * (n_rows // 2)
-        if side:
-            row = NG - row - n_rows // 2
-        return pl.ds(pl.multiple_of(row * LANES, LANES), part_cols)
-
-    def part_copy(half, side):
-        at = vol.at[1 - core_at, :, part_at(core_at, half, side)]
-        return remote(at, at, part_s.at[half, side], part_r.at[half, side], strip=mate)
-
-    def part_arrived(half, side):
-        at = vol.at[core_at, :, part_at(1 - core_at, half, side)]
-        return remote(at, at, part_s.at[half, side], part_r.at[half, side], strip=mate)
-
-    pl.loop(0, n_rows // 4)(project)
-    for side in range(2):
-        part_copy(0, side).start()
-
-    @pl.loop(1, n_angle)
-    def _(d):
-        ar_copy(d).wait()
-
-    summed = ar_in[0]
-    for a in range(1, n_angle):
-        summed = summed + ar_in[a]
-    ag_in[own_rows, :] = (summed * scale).astype(BF16)
-
-    def ag_copy(d):
-        peer = lax.rem(me_s + d, n_strip)
-        return remote(
-            ag_in.at[own_rows], ag_in.at[own_rows], ag_s.at[d], ag_r.at[d], strip=peer
-        )
-
-    @pl.loop(1, n_strip)
-    def _(d):
-        ag_copy(d).start()
-
-    pl.loop(n_rows // 4, n_rows // 2)(project)
-    for side in range(2):
-        part_copy(1, side).start()
+                vol[c, :, here] = total[group * 8 + k, c * 16 : c * 16 + 16]
+                vol[c, :, there] = turned[k * 32 + c * 16 : k * 32 + c * 16 + 16]
+        for side in range(2):
+            part_copy(group, side).start()
+            store_part(core_at, group, side, own_sem.at[group, side]).start()
 
     def ag_arrived(d):
         sender = lax.rem(me_s + n_strip - d, n_strip)
@@ -455,15 +473,21 @@
     pg_out[...] = ag_in[...].astype(F32)
     store_pg = pltpu.make_async_copy(pg_out, pg_hbm, store_sem.at[2])
     store_pg.start()
-    for half in range(2):
+    @pl.loop(0, n_groups)
+    def _(group):
         for side in range(2):
-            part_copy(half, side).wait_send()
-            part_arrived(half, side).wait_recv()
-    store_vol = pltpu.make_async_copy(vol.at[core_at], vol_hbm, store_sem.at[1])
-    store_vol.start()
+            part_arrived(group, side).wait_recv()
+            store_part(1 - core_at, group, side, mate_sem.at[group, side]).start()
+
+    @pl.loop(0, n_groups)
+    def _(group):
+        for side in range(2):
+            part_copy(group, side).wait_send()
+            store_part(core_at, group, side, own_sem.at[group, side]).wait()
+            store_part(1 - core_at, group, side, mate_sem.at[group, side]).wait()
+
     store_og.wait()
     store_pg.wait()
-    store_vol.wait()
 
 
 def shards(object_field, amplitudes, scan_offsets, probe_field, tilt_angles):
@@ -473,6 +497,7 @@
     trig = jnp.stack([jnp.cos(tilt_angles), jnp.sin(tilt_angles)])
     scale = 1.0 / math.sqrt(n_angle * n_strip * scan_offsets.shape[1])
     n_cols = WINDOW[1] - WINDOW[0]
+    parts = (NG // 32, 2)
     hbm = pl.BlockSpec(memory_space=pltpu.HBM)
     smem = pl.BlockSpec(memory_space=pltpu.SMEM)
     vmem, dma = pltpu.VMEM, pltpu.SemaphoreType.DMA
@@ -499,7 +524,7 @@
             vmem((2, FRAME, FRAME), F32),
             vmem((4, 4 * HALO, 2 * FRAME), BF16),
             vmem((4, 2 * FRAME, FRAME), BF16),
-            vmem((2 * FRAME, FRAME), F32),
+            vmem((4, 2 * FRAME, FRAME), F32),
             vmem((4, 2 * FRAME, FRAME), BF16),
             vmem((4, 4 * HALO, 2 * FRAME), BF16),
             vmem((4 * HALO, 2 * FRAME), F32),
@@ -510,17 +535,18 @@
             vmem((2, n_angle, 16, n_cols), BF16),
             vmem((2 * FRAME, FRAME), BF16),
             vmem((n_strip, 16, FRAME), BF16),
-            vmem((n_angle, 16, FRAME), F32),
+            vmem((n_angle, 16, FRAME), BF16),
             vmem((2 * FRAME, FRAME), BF16),
             vmem((2 * FRAME, FRAME), F32),
             vmem((n_angle, NG // 4, LANES), F32),
             vmem((n_angle, NG // 4, LANES), F32),
-            vmem((n_angle, 128, n_cols), BF16),
+            vmem((128, n_cols), BF16),
+            vmem((NG // 4, 64, LANES), F32),
             vmem((2, 16, NG * NG), F32),
             dma((5,)), dma((3,)), dma((2,)), dma((2,)), dma((2,)), dma((2,)),
             dma((n_angle,)), dma((n_angle,)), dma((n_strip,)), dma((n_strip,)),
             dma((n_angle,)), dma((n_angle,)), dma((n_strip,)), dma((n_strip,)),
-            dma((n_angle,)), dma((n_angle,)), dma((2, 2)), dma((2, 2)),
+            dma((n_angle,)), dma((n_angle,)), dma(parts), dma(parts), dma(parts), dma(parts),
         ],
         compiler_params=pltpu.CompilerParams(
             collective_id=0, has_side_effects=True, vmem_limit_bytes=60 * 1024 * 1024

time: 61.3 us -> 56.4 us (0.920)
  Pallas kernels: 55 us -> 49.8 us
    pallas_call x1, Pallas kernels: 55 us -> 49.8 us  [shards(): pl.pallas_call(lambda *refs: kernel(n_angle, n_strip, scale, *refs), out_...]
where the time goes in v3:
time: 56.4 us; the launch traced here: 55.9 us
  Pallas kernels  49.8 us (88%)
  local copies, waits for them, and re-layouts  4.88 us (9%)
  between operations  0.67 us (1%)
  other arithmetic  0.58 us (1%)
    pallas_call x1, Pallas kernels, shards(): pl.pallas_call(lambda *refs: kernel(n_angle, n_strip, scale, *refs), out_...  49.8 us
    unnamed x9, local copies, waits for them, and re-layouts  4.84 us

profile of v3, /device:TPU:1, one launch (start us, length us, event | category | flops | bytes accessed | tf_op | source)
XLA Modules:
  0.0 55.9 jit_solution(8112552911689117125)
XLA Ops:
  0.6 0.0 copy-start.2
  0.6 0.6 %copy-done.2 = f32[8]{0:T(128)S(1)} copy-done((f32[8]{0:T(128)S(1)}, f32[8]{0:T(128)}, u32[]{:S(2)}) %copy-start.2) | copy-done | bytes 56
  1.3 0.6 %pad_maximum_fusion.refs_1_ = f32[2,8]{1,0:T(2,128)} fusion(f32[1,8]{1,0:T(1,128)S(1)} %get-tuple-element.13, f32[1,8]{1,0:T(1,128)S(1)} %get-tuple-element.12), kind=kLoop, calls=%fused_computation | loop fusion | flops 16 | bytes 128 | tf_op jit(solution)/shard_map/stack | solution.py:497
  1.9 49.8 %gradient_step.1 = (f32[2,128,1024]{2,1,0:T(8,128)}, f32[512,256]{1,0:T(8,128)}, f32[16,16384]{1,0:T(8,128)}) custom-call(s32[1,2,4]{2,1,0:T(2,128)} %bitcast.17, f32[2,8]{1,0:T(2,128)} %pad_maximum_fusion.refs_1_, f32[2,128,1024]{2,1,0:T(8,128)} %bitcast.14, bf16[4,256,256]{2,1,0:T(8,128)(2,1)} %bitcast.16, f32[2,256,256]{2,1,0:T(8,128)} %refs_4_.1, ...), custom_call_target="tpu_custom_call" | custom-call | tf_op jit(solution)/shard_map/gradient_step/pallas_call | solution.py:504
  51.7 0.0 copy-start.1
  51.7 0.0 copy-start
  51.7 2.4 %copy.14 = f32[2,1,128,1024]{3,2,1,0:T(8,128)} copy(f32[2,1,128,1024]{3,2,1,0:T(8,128)} %bitcast.13) | data formatting | bytes 2097152
  54.2 0.0 copy-done.1
  54.2 0.8 %copy.15 = f32[2,256,256]{2,1,0:T(8,128)} copy(f32[2,256,256]{2,1,0:T(8,128)S(1)} %bitcast.15) | data formatting | bytes 1048576
  55.0 0.0 copy-done
  55.0 1.0 %copy.16 = f32[1,1,16,16384]{3,2,1,0:T(8,128)} copy(f32[1,1,16,16384]{3,2,1,0:T(8,128)S(1)} %bitcast.12) | data formatting | bytes 2097152
  (1 shorter events, 0.0 us)
Async XLA Ops:
  0.6 0.7 %copy-start.2 = (f32[8]{0:T(128)S(1)}, f32[8]{0:T(128)}, u32[]{:S(2)}) copy-start(f32[8]{0:T(128)} %param.11) | copy-start | bytes 100
  51.7 2.4 %copy-start.1 = (f32[512,256]{1,0:T(8,128)S(1)}, f32[512,256]{1,0:T(8,128)}, u32[]{:S(2)}) copy-start(f32[512,256]{1,0:T(8,128)} %get-tuple-element.7) | copy-start | bytes 1572868
  51.7 3.2 %copy-start = (f32[16,16384]{1,0:T(8,128)S(1)}, f32[16,16384]{1,0:T(8,128)}, u32[]{:S(2)}) copy-start(f32[16,16384]{1,0:T(8,128)} %get-tuple-element.8) | copy-start | bytes 3145732

commit v4 on v3

--- a/solution.py
+++ b/solution.py
@@ -37,9 +37,9 @@
     halo_out, halo_in, place_t, place_m, moved3, patch3, xbuf, ybuf, wbuf, mbuf, zbuf, gbuf,
     grad_out, grad_in, core, phase, ph_all,
     pterm, rs_in, ar_in, ag_in, pg_out,
-    lower_t, frac_t, lhs, total, vol,
+    lower_t, frac_t, lhs, total, vol, vol_in,
     load_sem, store_sem, halo_s, halo_r, grad_s, grad_r, a2a_s, a2a_r,
-    rs_s, rs_r, ar_s, ar_r, ag_s, ag_r, mate_s, mate_r, part_s, part_r, own_sem, mate_sem,
+    rs_s, rs_r, ar_s, ar_r, ag_s, ag_r, part_s, part_r, own_sem,
 ):
     width = ext.shape[2]
     me_a = lax.axis_index("angle")
@@ -73,6 +73,40 @@
             barrier, inc=1, device_id={"angle": lax.rem(me_a + d, n_angle)}, device_id_type=MESH
         )
 
+    def phase_sender(side, kind):
+        strip_to = me_s - core_at + side
+        if kind == 0:
+            return strip_to
+        neighbour = jnp.where(me_a >= n_angle // 2, strip_to + 1, strip_to + n_strip - 1)
+        return lax.rem(neighbour, n_strip)
+
+    def phase_target(kind, peer):
+        if kind == 0:
+            row, strip_to = HALO + peer * 16, me_s
+        else:
+            upper = peer >= n_angle // 2
+            row = jnp.where(upper, (peer - n_angle // 2) * 16, 3 * HALO + peer * 16)
+            strip_to = jnp.where(upper, above, below)
+        side = lax.rem(strip_to, 2)
+        return row, side, strip_to - side + lax.rem(me_a, 2)
+
+    @pl.loop(0, n_angle // 2)
+    def _(g):
+        a = 2 * g + core_at
+        for side in range(2):
+            for kind in range(2):
+                sender = phase_sender(side, kind)
+
+                @pl.when(jnp.logical_or(a != me_a, sender != me_s))
+                def _():
+                    pl.semaphore_signal(
+                        barrier, inc=1, device_id={"angle": a, "strip": sender}, device_id_type=MESH
+                    )
+
+    messages = 2 * n_angle
+    for kind in range(2):
+        messages = messages - jnp.where(phase_target(kind, me_a)[2] == me_s, 1, 0)
+
     loads[0].wait()
     for side, first in ((0, HALO), (1, 2 * HALO)):
 
@@ -84,7 +118,7 @@
                     part, pl.ds(first + rows, 16), :
                 ].astype(BF16)
 
-    pl.semaphore_wait(barrier, n_strip - 1 + n_angle - 1)
+    pl.semaphore_wait(barrier, n_strip - 1 + n_angle - 1 + messages)
 
     def remote(src, dst, send, recv, **where):
         return pltpu.make_async_remote_copy(
@@ -153,21 +187,21 @@
     exit_chunk(2)
 
     center = (NG - 1) / 2.0
-    n_rows = NG // 4
-    first_row = core_at * n_rows
+    n_rows = NG // 2
     shape = (n_rows, LANES)
-    xpos = (lax.broadcasted_iota(jnp.int32, shape, 0) + first_row).astype(F32) - center
+    xpos = lax.broadcasted_iota(jnp.int32, shape, 0).astype(F32) - center
     ypos = lax.broadcasted_iota(jnp.int32, shape, 1).astype(F32) - center
-
-    @pl.loop(0, n_angle)
-    def _(a):
+    n_turns = n_angle // 2
+
+    @pl.loop(0, n_turns)
+    def _(g):
+        a = 2 * g + core_at
         upos = (width - 1) / 2.0 + 2.0 * (xpos * trig[0, a] + ypos * trig[1, a])
         low = jnp.clip(jnp.floor(upos), 0.0, width - 2.0)
-        lower_t[a] = low - float(WINDOW[0])
-        total[pl.ds(a * (n_rows // n_angle), n_rows // n_angle)] = jnp.zeros(
-            (n_rows // n_angle, 64, LANES), F32
-        )
-        frac_t[a] = upos - low
+        lower_t[g] = low - float(WINDOW[0])
+        frac_t[g] = upos - low
+        each = n_rows // n_turns
+        total[pl.ds(g * each, each)] = jnp.zeros((each, 64, LANES), F32)
 
     for copy in halo_copies:
         copy.wait()
@@ -214,6 +248,8 @@
             blocks[b] = blocks[b] + terms[f][:, :LANES]
             blocks[b + 1] = blocks[b + 1] + terms[f][:, LANES:]
         return blocks
+
+    around = (WINDOW[0] // LANES * LANES, -(-WINDOW[1] // LANES) * LANES)
 
     def grad_chunk(chunk):
         gbuf[...] = jnp.dot(zbuf[chunk], fwd[...], preferred_element_type=F32)
@@ -246,24 +282,59 @@
                 q_im = q_im + (er * gi - ei * gr)
             pterm[pl.ds(row, 16), :] = q_re.astype(BF16)
             pterm[pl.ds(FRAME + row, 16), :] = q_im.astype(BF16)
-            for part, terms in ((0, t_re), (1, t_im)):
-                for b, value in enumerate(place(terms, moved3[part, pl.ds(local, 16), :])):
+            sums = [
+                place(terms, moved3[part, pl.ds(local, 16), :])
+                for part, terms in ((0, t_re), (1, t_im))
+            ]
+            for part in range(2):
+                for b, value in enumerate(sums[part]):
                     cols = slice(b * LANES, (b + 1) * LANES)
                     if chunk in (0, 3):
                         grad_out[chunk // 3, part, pl.ds(local, 16), cols] = value.astype(BF16)
                     else:
                         core[part, pl.ds((chunk - 1) * HALO + local, 16), cols] = value
-
-    grad_copies = [
-        remote(grad_out.at[1], grad_in.at[0], grad_s.at[0], grad_r.at[0], strip=below),
-        remote(grad_out.at[0], grad_in.at[1], grad_s.at[1], grad_r.at[1], strip=above),
-    ]
+            value = jnp.concatenate(
+                [
+                    ext[0, rows, b * LANES : (b + 1) * LANES] * sums[1][b]
+                    - ext[1, rows, b * LANES : (b + 1) * LANES] * sums[0][b]
+                    for b in range(around[0] // LANES, around[1] // LANES)
+                ],
+                axis=1,
+            )
+            value = pltpu.roll(value, around[1] - WINDOW[0], 1)
+            phase[rows, :] = value[:, : WINDOW[1] - WINDOW[0]].astype(BF16)
+
+    def phase_copy(kind, peer):
+        row, side, to = phase_target(kind, peer)
+        src = phase.at[pl.ds(pl.multiple_of(row, 16), 16)]
+        dst = ph_all.at[me_a // 2, side, kind]
+        copy = remote(
+            src, dst, a2a_s.at[kind, peer], a2a_r.at[me_a // 2, side, kind], angle=peer, strip=to
+        )
+        stays = jnp.logical_and(peer == me_a, to == me_s)
+        return copy, stays, src, dst
+
+    def send_phase(kind, first):
+        @pl.loop(first, first + n_angle // 2)
+        def _(peer):
+            copy, stays, src, dst = phase_copy(kind, peer)
+
+            @pl.when(stays)
+            def _():
+                dst[...] = src[...]
+
+            @pl.when(jnp.logical_not(stays))
+            def _():
+                copy.start()
+
     grad_chunk(0)
-    grad_copies[1].start()
+    send_phase(1, n_angle // 2)
     grad_chunk(3)
-    grad_copies[0].start()
+    send_phase(1, 0)
     grad_chunk(1)
+    send_phase(0, 0)
     grad_chunk(2)
+    send_phase(0, n_angle // 2)
 
     def rs_copy(d):
         peer = lax.rem(me_s + d, n_strip)
@@ -276,66 +347,14 @@
     def _(d):
         rs_copy(d).start()
 
-    around = (WINDOW[0] // LANES * LANES, -(-WINDOW[1] // LANES) * LANES)
+    grad_copies = [
+        remote(grad_out.at[1], grad_in.at[0], grad_s.at[0], grad_r.at[0], strip=below),
+        remote(grad_out.at[0], grad_in.at[1], grad_s.at[1], grad_r.at[1], strip=above),
+    ]
     for copy in grad_copies:
-        copy.wait()
-    for side, present in ((0, has_above), (1, has_below)):
-
-        @pl.loop(0, 4)
-        def _(step):
-            local = pl.multiple_of(step * 16, 16)
-            rows = pl.ds(side * HALO + local, 16)
-            got = [
-                core[part, rows, :]
-                + grad_in[side, part, pl.ds(local, 16), :].astype(F32) * present
-                for part in range(2)
-            ]
-            core[0, rows, :] = got[0]
-            core[1, rows, :] = got[1]
-            own = pl.ds(HALO + side * HALO + local, 16)
-            cut = slice(around[0], around[1])
-            value = ext[0, own, cut] * got[1][:, cut] - ext[1, own, cut] * got[0][:, cut]
-            value = pltpu.roll(value, around[1] - WINDOW[0], 1)
-            phase[rows, :] = value[:, : WINDOW[1] - WINDOW[0]].astype(BF16)
-
-    def farness(step):
-        near = (step + 1) // 2
-        return jnp.where(lax.rem(step, 2) == 1, near, lax.rem(n_angle - near, n_angle))
-
-    def a2a_copy(d):
-        peer = lax.rem(me_a + d, n_angle)
-        return remote(
-            phase.at[pl.ds(pl.multiple_of(peer * 16, 16), 16)], ph_all.at[core_at, me_a],
-            a2a_s.at[d], a2a_r.at[d], angle=peer,
-        )
-
-    def cross_copy(d):
-        peer = lax.rem(me_a + d, n_angle)
-        return remote(
-            phase.at[pl.ds(pl.multiple_of(peer * 16, 16), 16)], ph_all.at[core_at, me_a],
-            mate_s.at[d], mate_r.at[d], angle=peer, strip=mate,
-        )
-
-    @pl.loop(0, n_angle - 1)
-    def _(step):
-        d = farness(n_angle - 1 - step)
-        a2a_copy(d).start()
-        cross_copy(d).start()
-
-    cross_copy(0).start()
-    ph_all[core_at, me_a] = phase[pl.ds(pl.multiple_of(me_a * 16, 16), 16), :]
-
-    store_og = pltpu.make_async_copy(core, og_hbm, store_sem.at[0])
-    store_og.start()
-
-    @pl.loop(1, n_strip)
-    def _(d):
-        rs_copy(d).wait()
+        copy.start()
 
     own_rows = pl.ds(pl.multiple_of(me_s * 16, 16), 16)
-    ar_in[me_a] = lax.fori_loop(
-        1, n_strip, lambda d, acc: acc + rs_in[d].astype(F32), pterm[own_rows, :].astype(F32)
-    ).astype(BF16)
 
     def ar_copy(d):
         peer = lax.rem(me_a + d, n_angle)
@@ -343,9 +362,36 @@
             ar_in.at[me_a], ar_in.at[me_a], ar_s.at[d], ar_r.at[d], angle=peer
         )
 
-    @pl.loop(1, n_angle)
-    def _(d):
-        ar_copy(d).start()
+    store_og = pltpu.make_async_copy(core, og_hbm, store_sem.at[0])
+
+    def finish_object():
+        for copy in grad_copies:
+            copy.wait()
+        for side, present in ((0, has_above), (1, has_below)):
+
+            @pl.loop(0, 4)
+            def _(step):
+                local = pl.multiple_of(step * 16, 16)
+                rows = pl.ds(side * HALO + local, 16)
+                for part in range(2):
+                    core[part, rows, :] += (
+                        grad_in[side, part, pl.ds(local, 16), :].astype(F32) * present
+                    )
+
+        store_og.start()
+
+    def exchange_probe():
+        @pl.loop(1, n_strip)
+        def _(d):
+            rs_copy(d).wait()
+
+        ar_in[me_a] = lax.fori_loop(
+            1, n_strip, lambda d, acc: acc + rs_in[d].astype(F32), pterm[own_rows, :].astype(F32)
+        ).astype(BF16)
+
+        @pl.loop(1, n_angle)
+        def _(d):
+            ar_copy(d).start()
 
     flip = (
         lax.broadcasted_iota(jnp.int32, (LANES, LANES), 0)
@@ -376,8 +422,8 @@
         def _(d):
             ag_copy(d).start()
 
-    def one_hot(a, i):
-        low = lower_t[a, pl.ds(i, 1), :]
+    def one_hot(g, i):
+        low = lower_t[g, pl.ds(i, 1), :]
         return jnp.concatenate(
             [
                 jnp.where(column == (low - float(j)).astype(BF16), one, zero)
@@ -386,25 +432,73 @@
             axis=0,
         )
 
-    def project(a, pair):
-        picks = jnp.concatenate([one_hot(a, 2 * pair + k) for k in range(2)], axis=1)
+    def project(g, pair):
+        picks = jnp.concatenate([one_hot(g, 2 * pair + k) for k in range(2)], axis=1)
         got = jnp.dot(lhs[...], picks, preferred_element_type=F32)
         for k in range(2):
-            frac = frac_t[a, pl.ds(2 * pair + k, 1), :]
+            frac = frac_t[g, pl.ds(2 * pair + k, 1), :]
             part = got[:, k * LANES : (k + 1) * LANES]
             total[2 * pair + k] += part[:64] * (1.0 - frac) + part[64:] * frac
 
-    @pl.loop(0, n_angle)
+    n_groups = n_rows // 16
+    group_cols = 16 * LANES
+
+    def group_at(group, side):
+        row = group * 16
+        if side:
+            row = NG - row - 16
+        return pl.ds(pl.multiple_of(row * LANES, LANES), group_cols)
+
+    def part_copy(group, side):
+        cols = group_at(group, side)
+        return remote(
+            vol.at[1 - core_at, :, cols], vol_in.at[:, cols],
+            part_s.at[group, side], part_r.at[group, side], strip=mate,
+        )
+
+    def store_part(group, side):
+        cols = group_at(group, side)
+        return pltpu.make_async_copy(
+            vol.at[core_at, :, cols], vol_hbm.at[:, cols], own_sem.at[group, side]
+        )
+
+    def finish_group(group):
+        stack = jnp.concatenate([total[group * 16 + k, 32:] for k in range(16)], axis=0)
+        turned = joined(jnp.dot(split(stack), flip, preferred_element_type=F32))
+        for k in range(16):
+            x = group * 16 + k
+            here = pl.ds(pl.multiple_of(x * LANES, LANES), LANES)
+            there = pl.ds(pl.multiple_of((NG - 1 - x) * LANES, LANES), LANES)
+            for c in range(2):
+                vol[c, :, here] = total[x, c * 16 : c * 16 + 16]
+                vol[c, :, there] = turned[k * 32 + c * 16 : k * 32 + c * 16 + 16]
+        for side in range(2):
+            part_copy(group, side).start()
+
+    same = lax.rem(me_a + core_at, 2) == 0
+
+    @pl.loop(0, n_turns)
     def _(step):
-        d = farness(step)
-        a = lax.rem(me_a + n_angle - d, n_angle)
-
-        @pl.when(step > 0)
-        def _():
-            a2a_copy(d).wait()
-
-        cross_copy(d).wait()
-        rows = jnp.concatenate([ph_all[0, a], ph_all[1, a]], axis=0)
+        odd = lax.rem(step, 2)
+        even_far = jnp.where(odd == 1, step + 1, n_angle - step)
+        odd_far = jnp.where(odd == 1, n_angle - step, step + 1)
+        a = lax.rem(me_a + jnp.where(same, even_far, odd_far), n_angle)
+        g = a // 2
+        for side in range(2):
+            for kind in range(2):
+                sender = phase_sender(side, kind)
+                dst = ph_all.at[g, side, kind]
+
+                @pl.when(jnp.logical_or(a != me_a, sender != me_s))
+                def _():
+                    remote(
+                        dst, dst, a2a_s.at[kind, 0], a2a_r.at[g, side, kind], strip=mate
+                    ).wait_recv()
+
+        rows = jnp.concatenate(
+            [ph_all[g, side, 0].astype(F32) + ph_all[g, side, 1].astype(F32) for side in range(2)],
+            axis=0,
+        ).astype(BF16)
         mirrored = [
             jnp.dot(rows[:, b : b + LANES], flip, preferred_element_type=F32)
             for b in range(0, n_cols, LANES)
@@ -415,50 +509,43 @@
         lhs[:64, :] = both.astype(BF16)
         lhs[64:, :] = pltpu.roll(both, n_cols - 1, 1).astype(BF16)
 
-        @pl.loop(0, n_rows // 16)
+        @pl.loop(0, n_groups)
         def _(group):
             for pair in range(8):
-                project(a, group * 8 + pair)
-
-        @pl.when(step == n_angle - 2)
+                project(g, group * 8 + pair)
+
+            @pl.when(step == n_turns - 1)
+            def _():
+                finish_group(group)
+
+        @pl.when(step == 0)
+        def _():
+            exchange_probe()
+
+        @pl.when(step == 1)
+        def _():
+            finish_object()
+
+        @pl.when(step == n_turns - 2)
         def _():
             gather_probe()
 
-    n_groups = n_rows // 8
-    group_cols = 8 * LANES
-
-    def group_at(owner, group, side):
-        row = owner * n_rows + group * 8
-        if side:
-            row = NG - row - 8
-        return pl.ds(pl.multiple_of(row * LANES, LANES), group_cols)
-
-    def part_copy(group, side):
-        at = vol.at[1 - core_at, :, group_at(core_at, group, side)]
-        return remote(at, at, part_s.at[group, side], part_r.at[group, side], strip=mate)
-
-    def part_arrived(group, side):
-        at = vol.at[core_at, :, group_at(1 - core_at, group, side)]
-        return remote(at, at, part_s.at[group, side], part_r.at[group, side], strip=mate)
-
-    def store_part(owner, group, side, sem):
-        cols = group_at(owner, group, side)
-        return pltpu.make_async_copy(vol.at[core_at, :, cols], vol_hbm.at[:, cols], sem)
+    @pl.loop(0, n_angle)
+    def _(peer):
+        for kind in range(2):
+            copy, stays, _, _ = phase_copy(kind, peer)
+
+            @pl.when(jnp.logical_not(stays))
+            def _():
+                copy.wait_send()
 
     @pl.loop(0, n_groups)
     def _(group):
-        stack = jnp.concatenate([total[group * 8 + k, 32:] for k in range(8)], axis=0)
-        turned = joined(jnp.dot(split(stack), flip, preferred_element_type=F32))
-        for k in range(8):
-            x = first_row + group * 8 + k
-            here = pl.ds(pl.multiple_of(x * LANES, LANES), LANES)
-            there = pl.ds(pl.multiple_of((NG - 1 - x) * LANES, LANES), LANES)
-            for c in range(2):
-                vol[c, :, here] = total[group * 8 + k, c * 16 : c * 16 + 16]
-                vol[c, :, there] = turned[k * 32 + c * 16 : k * 32 + c * 16 + 16]
         for side in range(2):
-            part_copy(group, side).start()
-            store_part(core_at, group, side, own_sem.at[group, side]).start()
+            part_copy(group, side).wait_recv()
+            cols = group_at(group, side)
+            vol[core_at, :, cols] += vol_in[:, cols]
+            store_part(group, side).start()
 
     def ag_arrived(d):
         sender = lax.rem(me_s + n_strip - d, n_strip)
@@ -476,15 +563,8 @@
     @pl.loop(0, n_groups)
     def _(group):
         for side in range(2):
-            part_arrived(group, side).wait_recv()
-            store_part(1 - core_at, group, side, mate_sem.at[group, side]).start()
-
-    @pl.loop(0, n_groups)
-    def _(group):
-        for side in range(2):
             part_copy(group, side).wait_send()
-            store_part(core_at, group, side, own_sem.at[group, side]).wait()
-            store_part(1 - core_at, group, side, mate_sem.at[group, side]).wait()
+            store_part(group, side).wait()
 
     store_og.wait()
     store_pg.wait()
@@ -531,22 +611,23 @@
             vmem((2, 2, HALO, width), BF16),
             vmem((2, 2, HALO, width), BF16),
             vmem((2, 128, width), F32),
-            vmem((128, n_cols), BF16),
-            vmem((2, n_angle, 16, n_cols), BF16),
+            vmem((FRAME, n_cols), BF16),
+            vmem((n_angle // 2, 2, 2, 16, n_cols), BF16),
             vmem((2 * FRAME, FRAME), BF16),
             vmem((n_strip, 16, FRAME), BF16),
             vmem((n_angle, 16, FRAME), BF16),
             vmem((2 * FRAME, FRAME), BF16),
             vmem((2 * FRAME, FRAME), F32),
-            vmem((n_angle, NG // 4, LANES), F32),
-            vmem((n_angle, NG // 4, LANES), F32),
+            vmem((n_angle // 2, NG // 2, LANES), F32),
+            vmem((n_angle // 2, NG // 2, LANES), F32),
             vmem((128, n_cols), BF16),
-            vmem((NG // 4, 64, LANES), F32),
+            vmem((NG // 2, 64, LANES), F32),
             vmem((2, 16, NG * NG), F32),
+            vmem((16, NG * NG), F32),
             dma((5,)), dma((3,)), dma((2,)), dma((2,)), dma((2,)), dma((2,)),
+            dma((2, n_angle)), dma((n_angle // 2, 2, 2)), dma((n_strip,)), dma((n_strip,)),
             dma((n_angle,)), dma((n_angle,)), dma((n_strip,)), dma((n_strip,)),
-            dma((n_angle,)), dma((n_angle,)), dma((n_strip,)), dma((n_strip,)),
-            dma((n_angle,)), dma((n_angle,)), dma(parts), dma(parts), dma(parts), dma(parts),
+            dma(parts), dma(parts), dma(parts),
         ],
         compiler_params=pltpu.CompilerParams(
             collective_id=0, has_side_effects=True, vmem_limit_bytes=60 * 1024 * 1024

time: 56.4 us -> 52.2 us (0.926)
  Pallas kernels: 49.8 us -> 45.9 us
    pallas_call x1, Pallas kernels: 49.8 us -> 45.9 us  [shards(): pl.pallas_call(lambda *refs: kernel(n_angle, n_strip, scale, *refs), out_...]
where the time goes in v4:
time: 52.2 us; the launch traced here: 52.1 us
  Pallas kernels  45.9 us (88%)
  local copies, waits for them, and re-layouts  4.88 us (9%)
  between operations  0.67 us (1%)
  other arithmetic  0.58 us (1%)
    pallas_call x1, Pallas kernels, shards(): pl.pallas_call(lambda *refs: kernel(n_angle, n_strip, scale, *refs), out_...  45.9 us
    unnamed x9, local copies, waits for them, and re-layouts  4.84 us

profile of v4, /device:TPU:1, one launch (start us, length us, event | category | flops | bytes accessed | tf_op | source)
XLA Modules:
  0.0 52.1 jit_solution(1720302092398330653)
XLA Ops:
  0.6 0.0 copy-start.2
  0.6 0.6 %copy-done.2 = f32[8]{0:T(128)S(1)} copy-done((f32[8]{0:T(128)S(1)}, f32[8]{0:T(128)}, u32[]{:S(2)}) %copy-start.2) | copy-done | bytes 56
  1.3 0.6 %pad_maximum_fusion.refs_1_ = f32[2,8]{1,0:T(2,128)} fusion(f32[1,8]{1,0:T(1,128)S(1)} %get-tuple-element.13, f32[1,8]{1,0:T(1,128)S(1)} %get-tuple-element.12), kind=kLoop, calls=%fused_computation | loop fusion | flops 16 | bytes 128 | tf_op jit(solution)/shard_map/stack | solution.py:577
  1.9 45.9 %gradient_step.1 = (f32[2,128,1024]{2,1,0:T(8,128)}, f32[512,256]{1,0:T(8,128)}, f32[16,16384]{1,0:T(8,128)}) custom-call(s32[1,2,4]{2,1,0:T(2,128)} %bitcast.17, f32[2,8]{1,0:T(2,128)} %pad_maximum_fusion.refs_1_, f32[2,128,1024]{2,1,0:T(8,128)} %bitcast.14, bf16[4,256,256]{2,1,0:T(8,128)(2,1)} %bitcast.16, f32[2,256,256]{2,1,0:T(8,128)} %refs_4_.1, ...), custom_call_target="tpu_custom_call" | custom-call | tf_op jit(solution)/shard_map/gradient_step/pallas_call | solution.py:584
  47.9 0.0 copy-start.1
  47.9 0.0 copy-start
  47.9 2.4 %copy.14 = f32[2,1,128,1024]{3,2,1,0:T(8,128)} copy(f32[2,1,128,1024]{3,2,1,0:T(8,128)} %bitcast.13) | data formatting | bytes 2097152
  50.3 0.0 copy-done.1
  50.3 0.8 %copy.15 = f32[2,256,256]{2,1,0:T(8,128)} copy(f32[2,256,256]{2,1,0:T(8,128)S(1)} %bitcast.15) | data formatting | bytes 1048576
  51.1 0.0 copy-done
  51.1 1.0 %copy.16 = f32[1,1,16,16384]{3,2,1,0:T(8,128)} copy(f32[1,1,16,16384]{3,2,1,0:T(8,128)S(1)} %bitcast.12) | data formatting | bytes 2097152
  (1 shorter events, 0.0 us)
Async XLA Ops:
  0.6 0.7 %copy-start.2 = (f32[8]{0:T(128)S(1)}, f32[8]{0:T(128)}, u32[]{:S(2)}) copy-start(f32[8]{0:T(128)} %param.11) | copy-start | bytes 100
  47.9 2.4 %copy-start.1 = (f32[512,256]{1,0:T(8,128)S(1)}, f32[512,256]{1,0:T(8,128)}, u32[]{:S(2)}) copy-start(f32[512,256]{1,0:T(8,128)} %get-tuple-element.7) | copy-start | bytes 1572868
  47.9 3.2 %copy-start = (f32[16,16384]{1,0:T(8,128)S(1)}, f32[16,16384]{1,0:T(8,128)}, u32[]{:S(2)}) copy-start(f32[16,16384]{1,0:T(8,128)} %get-tuple-element.8) | copy-start | bytes 3145732

commit v5 on v4

--- a/solution.py
+++ b/solution.py
@@ -61,7 +61,9 @@
 
     barrier = pltpu.get_barrier_semaphore()
 
-    @pl.loop(1, n_strip)
+    pl.semaphore_signal(barrier, inc=1, device_id={"strip": above}, device_id_type=MESH)
+
+    @pl.loop(1, n_strip - 1)
     def _(d):
         pl.semaphore_signal(
             barrier, inc=1, device_id={"strip": lax.rem(me_s + d, n_strip)}, device_id_type=MESH
@@ -522,11 +524,11 @@
         def _():
             exchange_probe()
 
-        @pl.when(step == 1)
+        @pl.when(step == n_turns - 1)
         def _():
             finish_object()
 
-        @pl.when(step == n_turns - 2)
+        @pl.when(step == 1)
         def _():
             gather_probe()
 

time: 52.2 us -> 53.1 us (1.017)
  Pallas kernels: 45.9 us -> 46.9 us
    pallas_call x1, Pallas kernels: 45.9 us -> 46.9 us  [shards(): pl.pallas_call(lambda *refs: kernel(n_angle, n_strip, scale, *refs), out_...]
where the time goes in v5:
time: 53.1 us; the launch traced here: 53 us
  Pallas kernels  46.9 us (88%)
  local copies, waits for them, and re-layouts  4.88 us (9%)
  between operations  0.67 us (1%)
  other arithmetic  0.58 us (1%)
    pallas_call x1, Pallas kernels, shards(): pl.pallas_call(lambda *refs: kernel(n_angle, n_strip, scale, *refs), out_...  46.9 us
    unnamed x9, local copies, waits for them, and re-layouts  4.84 us

profile of v5, /device:TPU:1, one launch (start us, length us, event | category | flops | bytes accessed | tf_op | source)
XLA Modules:
  0.0 53.0 jit_solution(11826491492490887350)
XLA Ops:
  0.6 0.0 copy-start.2
  0.6 0.6 %copy-done.2 = f32[8]{0:T(128)S(1)} copy-done((f32[8]{0:T(128)S(1)}, f32[8]{0:T(128)}, u32[]{:S(2)}) %copy-start.2) | copy-done | bytes 56
  1.3 0.6 %pad_maximum_fusion.refs_1_ = f32[2,8]{1,0:T(2,128)} fusion(f32[1,8]{1,0:T(1,128)S(1)} %get-tuple-element.13, f32[1,8]{1,0:T(1,128)S(1)} %get-tuple-element.12), kind=kLoop, calls=%fused_computation | loop fusion | flops 16 | bytes 128 | tf_op jit(solution)/shard_map/stack | solution.py:579
  1.9 46.9 %gradient_step.1 = (f32[2,128,1024]{2,1,0:T(8,128)}, f32[512,256]{1,0:T(8,128)}, f32[16,16384]{1,0:T(8,128)}) custom-call(s32[1,2,4]{2,1,0:T(2,128)} %bitcast.17, f32[2,8]{1,0:T(2,128)} %pad_maximum_fusion.refs_1_, f32[2,128,1024]{2,1,0:T(8,128)} %bitcast.14, bf16[4,256,256]{2,1,0:T(8,128)(2,1)} %bitcast.16, f32[2,256,256]{2,1,0:T(8,128)} %refs_4_.1, ...), custom_call_target="tpu_custom_call" | custom-call | tf_op jit(solution)/shard_map/gradient_step/pallas_call | solution.py:586
  48.8 0.0 copy-start.1
  48.8 0.0 copy-start
  48.8 2.4 %copy.14 = f32[2,1,128,1024]{3,2,1,0:T(8,128)} copy(f32[2,1,128,1024]{3,2,1,0:T(8,128)} %bitcast.13) | data formatting | bytes 2097152
  51.2 0.0 copy-done.1
  51.2 0.8 %copy.15 = f32[2,256,256]{2,1,0:T(8,128)} copy(f32[2,256,256]{2,1,0:T(8,128)S(1)} %bitcast.15) | data formatting | bytes 1048576
  52.0 0.0 copy-done
  52.0 1.0 %copy.16 = f32[1,1,16,16384]{3,2,1,0:T(8,128)} copy(f32[1,1,16,16384]{3,2,1,0:T(8,128)S(1)} %bitcast.12) | data formatting | bytes 2097152
  (1 shorter events, 0.0 us)
Async XLA Ops:
  0.6 0.7 %copy-start.2 = (f32[8]{0:T(128)S(1)}, f32[8]{0:T(128)}, u32[]{:S(2)}) copy-start(f32[8]{0:T(128)} %param.11) | copy-start | bytes 100
  48.8 2.4 %copy-start.1 = (f32[512,256]{1,0:T(8,128)S(1)}, f32[512,256]{1,0:T(8,128)}, u32[]{:S(2)}) copy-start(f32[512,256]{1,0:T(8,128)} %get-tuple-element.7) | copy-start | bytes 1572868
  48.8 3.2 %copy-start = (f32[16,16384]{1,0:T(8,128)S(1)}, f32[16,16384]{1,0:T(8,128)}, u32[]{:S(2)}) copy-start(f32[16,16384]{1,0:T(8,128)} %get-tuple-element.8) | copy-start | bytes 3145732

commit v6 on v5

--- a/solution.py
+++ b/solution.py
@@ -570,6 +570,31 @@
 
     store_og.wait()
     store_pg.wait()
+
+
+def deliver(object_in, probe_in, volume_in, object_out, probe_out, volume_out,
+            object_buf, probe_buf, volume_buf, in_sem, out_sem):
+    loads, stores = [], []
+    for part in range(4):
+        half = (part // 2, pl.ds(part % 2 * 64, 64))
+        rows = pl.ds(part * 128, 128)
+        cols = (slice(None), pl.ds(part * 4096, 4096))
+        for i, (src, buf, dst, at) in enumerate(
+            (
+                (object_in, object_buf, object_out, half),
+                (volume_in, volume_buf, volume_out, cols),
+                (probe_in, probe_buf, probe_out, rows),
+            )
+        ):
+            loads.append(pltpu.make_async_copy(src.at[at], buf.at[at], in_sem.at[i, part]))
+            stores.append(pltpu.make_async_copy(buf.at[at], dst.at[at], out_sem.at[i, part]))
+    for load in loads:
+        load.start()
+    for load, store in zip(loads, stores):
+        load.wait()
+        store.start()
+    for store in stores:
+        store.wait()
 
 
 def shards(object_field, amplitudes, scan_offsets, probe_field, tilt_angles):
@@ -638,6 +663,16 @@
     )(
         scan_offsets.transpose(0, 2, 1), trig, object_field[:, 0], amplitudes[0], probe_field, fwd, inv
     )
+    results = (object_grad, probe_grad, volume)
+    object_grad, probe_grad, volume = pl.pallas_call(
+        deliver,
+        out_shape=tuple(jax.ShapeDtypeStruct(r.shape, r.dtype) for r in results),
+        in_specs=[hbm] * 3,
+        out_specs=(hbm,) * 3,
+        scratch_shapes=[vmem(r.shape, r.dtype) for r in results] + [dma((3, 4)), dma((3, 4))],
+        compiler_params=pltpu.CompilerParams(vmem_limit_bytes=60 * 1024 * 1024),
+        name="deliver",
+    )(*results)
     return (
         object_grad[:, None],
         probe_grad.reshape(2, FRAME, FRAME),

time: 53.1 us -> 51.6 us (0.972)
  local copies, waits for them, and re-layouts: 4.88 us -> 0.69 us
  Pallas kernels: 46.9 us -> 49.5 us
    unnamed x9 -> x2, local copies, waits for them, and re-layouts: 4.84 us -> 0.65 us
    pallas_call x0 -> x1, Pallas kernels: none -> 2.63 us  [shards(): pl.pallas_call(deliver, out_shape=tuple((jax.ShapeDtypeStruct(r.shape, r....]
where the time goes in v6:
time: 51.6 us; the launch traced here: 51.4 us
  Pallas kernels  49.5 us (96%)
  local copies, waits for them, and re-layouts  0.69 us (1%)
  between operations  0.65 us (1%)
  other arithmetic  0.58 us (1%)
    pallas_call x1, Pallas kernels, shards(): pl.pallas_call(lambda *refs: kernel(n_angle, n_strip, scale, *refs), out_...  46.9 us
    pallas_call x1, Pallas kernels, shards(): pl.pallas_call(deliver, out_shape=tuple((jax.ShapeDtypeStruct(r.shape, r....  2.63 us

profile of v6, /device:TPU:1, one launch (start us, length us, event | category | flops | bytes accessed | tf_op | source)
XLA Modules:
  0.0 51.4 jit_solution(8364511720462423733)
XLA Ops:
  0.6 0.0 copy-start
  0.6 0.6 %copy-done = f32[8]{0:T(128)S(1)} copy-done((f32[8]{0:T(128)S(1)}, f32[8]{0:T(128)}, u32[]{:S(2)}) %copy-start) | copy-done | bytes 56
  1.3 0.6 %pad_maximum_fusion.refs_1_ = f32[2,8]{1,0:T(2,128)} fusion(f32[1,8]{1,0:T(1,128)S(1)} %get-tuple-element.19, f32[1,8]{1,0:T(1,128)S(1)} %get-tuple-element.18), kind=kLoop, calls=%fused_computation | loop fusion | flops 16 | bytes 128 | tf_op jit(solution)/shard_map/stack | solution.py:604
  1.9 46.9 %gradient_step.1 = (f32[2,128,1024]{2,1,0:T(8,128)}, f32[512,256]{1,0:T(8,128)}, f32[16,16384]{1,0:T(8,128)}) custom-call(s32[1,2,4]{2,1,0:T(2,128)} %bitcast.14, f32[2,8]{1,0:T(2,128)} %pad_maximum_fusion.refs_1_, f32[2,128,1024]{2,1,0:T(8,128)} %bitcast.12, bf16[4,256,256]{2,1,0:T(8,128)(2,1)} %bitcast.13, f32[2,256,256]{2,1,0:T(8,128)} %refs_4_.1, ...), custom_call_target="tpu_custom_call" | custom-call | tf_op jit(solution)/shard_map/gradient_step/pallas_call | solution.py:611
  48.8 2.6 %deliver.1 = (f32[2,128,1024]{2,1,0:T(8,128)}, f32[512,256]{1,0:T(8,128)}, f32[16,16384]{1,0:T(8,128)}) custom-call(f32[2,128,1024]{2,1,0:T(8,128)} %get-tuple-element.9.object_in, f32[512,256]{1,0:T(8,128)} %get-tuple-element.10.probe_in, f32[16,16384]{1,0:T(8,128)} %get-tuple-element.11.volume_in), custom_call_target="tpu_custom_call" | custom-call | tf_op jit(solution)/shard_map/deliver/pallas_call | solution.py:667
  (1 shorter events, 0.0 us)
Async XLA Ops:
  0.6 0.7 %copy-start = (f32[8]{0:T(128)S(1)}, f32[8]{0:T(128)}, u32[]{:S(2)}) copy-start(f32[8]{0:T(128)} %param.11) | copy-start | bytes 100
